TPU v7x, 32 devices: a whole 2x2x4 slice. The times are simulated.
32 devices in a mesh: dp: 8 (over z, y), grp: 4 (over x, core).
Axes of the slice: x: 2, y: 2, z: 4, core: 2. Of those that a mesh axis runs over, the one named last changes fastest.
Arguments:
- clips: bfloat16 [8192, 1024], P(('dp', 'grp')), may hold values from -6 to 6
- captions: bfloat16 [128, 1024], P(('dp', 'grp')), may hold values from -6 to 6
- clip_group: int32 [8192], P(('dp', 'grp')), may hold values from 0 to 31, as said below
- caption_group: int32 [128], P(('dp', 'grp')), may hold values from 0 to 31, as said below
Outputs:
- clip_grad: float32 [8192, 1024], P(('dp', 'grp'))
- group_loss: float32 [32], P('grp')
Inputs may be any that keep to these rules, and one draw needn't show every extreme that they name: `clip_group`: every group has at least one clip. `caption_group`: every group has at least two captions.
All inputs are finite; a program needn't handle non-finite values.
Results may differ from a plain program's by a relative error of at most 0.0028.
Values may be sent and summed in bfloat16 or wider, within the bound.
No kernel may reach another device: no remote copies, remote signals or barrier semaphores. Data moves between devices by JAX's collectives and lax.ppermute only.
A program may use at most 64 MiB of HBM per device.

v0:
```python
import math

import jax
import jax.numpy as jnp
from jax import lax
from jax.sharding import PartitionSpec as P

NEGATIVE = -1e30


def merged(part, axis, combine):
    gathered = jax.tree.map(lambda a: lax.all_gather(a, axis), part)

    def take(source):
        return jax.tree.map(lambda a: lax.dynamic_index_in_dim(a, source, 0, False), gathered)

    return lax.fori_loop(
        1, lax.axis_size(axis), lambda source, state: combine(state, take(source)), take(0)
    )


def merge_pair(left_side, right_side):
    top_all = jnp.maximum(left_side[0], right_side[0])
    denominator = left_side[1] * jnp.exp(left_side[0] - top_all) + right_side[1] * jnp.exp(
        right_side[0] - top_all
    )
    top_pos = jnp.maximum(left_side[2], right_side[2])
    numerator = left_side[3] * jnp.exp(left_side[2] - top_pos) + right_side[3] * jnp.exp(
        right_side[2] - top_pos
    )
    return (top_all, denominator, top_pos, numerator)


def lookup(onehot, first_col, second_col):
    return jnp.dot(
        onehot, jnp.stack([first_col, second_col], axis=1), precision=lax.Precision.HIGHEST
    )


def group_totals(onehot, first_col, second_col):
    values = jnp.stack([first_col, second_col], axis=1)
    return lax.dot_general(
        onehot, values, (((0,), (0,)), ((), ())), precision=lax.Precision.HIGHEST
    )


def shards(clips, captions, clip_group, caption_group):
    clip_rows = clips.shape[0]
    feat_width = clips.shape[1]
    devices_all = lax.axis_size("dp") * lax.axis_size("grp")
    groups = captions.shape[0] * devices_all // 4
    nclips_all = clip_rows * devices_all
    factor = 3.0 / math.sqrt(feat_width)

    def absorb(state_now, block_pair):
        row_max, row_sum, pos_max, pos_sum, mixed_sums = state_now
        block_caps, block_ids = block_pair
        scores = (
            lax.dot_general(
                clips, block_caps, (((1,), (1,)), ((), ())), preferred_element_type=jnp.float32
            )
            * factor
        )
        new_max = jnp.maximum(row_max, jnp.max(scores, axis=1))
        weights = jnp.exp(scores - new_max[:, None])
        positive = clip_group[:, None] == block_ids[None, :]
        masked = jnp.where(positive, scores, NEGATIVE)
        new_pos = jnp.maximum(pos_max, jnp.max(masked, axis=1))
        pos_weights = jnp.where(positive, jnp.exp(masked - new_pos[:, None]), 0.0)
        keep_all = jnp.exp(row_max - new_max)
        keep_pos = jnp.exp(pos_max - new_pos)
        stacked = jnp.concatenate([weights, pos_weights], axis=0).astype(jnp.bfloat16)
        update = jnp.dot(stacked, block_caps, preferred_element_type=jnp.float32)
        mixed_sums = mixed_sums * jnp.concatenate([keep_all, keep_pos])[:, None] + update
        return (
            (
                new_max,
                row_sum * keep_all + jnp.sum(weights, axis=1),
                new_pos,
                pos_sum * keep_pos + jnp.sum(pos_weights, axis=1),
                mixed_sums,
            ),
            None,
        )

    start_state = (
        jnp.full((clip_rows,), NEGATIVE, jnp.float32),
        jnp.zeros((clip_rows,), jnp.float32),
        jnp.full((clip_rows,), NEGATIVE, jnp.float32),
        jnp.zeros((clip_rows,), jnp.float32),
        jnp.zeros((2 * clip_rows, feat_width), jnp.float32),
    )
    all_caps, all_ids = (
        lax.all_gather(captions, ("dp", "grp"), axis=0, tiled=True),
        lax.all_gather(caption_group, ("dp", "grp"), axis=0, tiled=True),
    )
    total_caps = all_caps.shape[0]
    block_cols = 512 if total_caps % 512 == 0 else total_caps
    block_count = total_caps // block_cols
    folded, unused = lax.scan(
        absorb,
        start_state,
        (
            all_caps.reshape(block_count, block_cols, feat_width),
            all_ids.reshape(block_count, block_cols),
        ),
    )
    row_max, row_sum, pos_max, pos_sum, mixed_sums = folded
    member = clip_group[:, None] == jnp.arange(groups, dtype=jnp.int32)[None, :]
    onehot = member.astype(jnp.float32)
    local_top = jnp.max(jnp.where(member, row_max[:, None], NEGATIVE), axis=0)
    local_pos_top = jnp.max(jnp.where(member, pos_max[:, None], NEGATIVE), axis=0)
    own_share = groups // lax.axis_size("grp")
    offset = lax.axis_index("grp") * own_share
    picked_local = lookup(onehot, local_top, local_pos_top)
    local_lift = jnp.exp(row_max - picked_local[:, 0])
    local_pos_lift = jnp.exp(pos_max - picked_local[:, 1])
    group_sums = group_totals(onehot, local_lift * row_sum, local_pos_lift * pos_sum)
    top_all, denominator, top_pos, numerator = merged(
        (local_top, group_sums[:, 0], local_pos_top, group_sums[:, 1]), ("dp", "grp"), merge_pair
    )
    picked = lookup(onehot, top_all, top_pos)
    lift_all = jnp.exp(row_max - picked[:, 0])
    lift_pos = jnp.exp(pos_max - picked[:, 1])
    full_loss = top_all + jnp.log(denominator) - (top_pos + jnp.log(numerator))
    group_loss = lax.dynamic_slice_in_dim(full_loss, offset, own_share)
    factors = lookup(onehot, 1.0 / denominator, 1.0 / numerator)
    gain_all = lift_all * factors[:, 0]
    gain_pos = lift_pos * factors[:, 1]
    clip_grad = (
        nclips_all
        / groups
        * (gain_all[:, None] * mixed_sums[:clip_rows] - gain_pos[:, None] * mixed_sums[clip_rows:])
    )
    return (clip_grad, group_loss)


def solution(mesh):
    return jax.shard_map(
        shards,
        mesh=mesh,
        in_specs=(
            P(("dp", "grp"), None),
            P(("dp", "grp"), None),
            P(("dp", "grp")),
            P(("dp", "grp")),
        ),
        out_specs=(P(("dp", "grp"), None), P("grp")),
        check_vma=False,
    )
```

profile of v0, /device:TPU:0, one launch (start us, length us, event | category | flops | bytes accessed | tf_op | source)
XLA Modules:
  0.0 130.5 jit_solution(6697435109317320846)
XLA Ops:
  0.7 0.9 dynamic-update-slice.1
  1.6 42.0 %all-reduce.1 = s32[128]{0:T(128)S(1)} all-reduce(s32[128]{0:T(128)S(1)} %dynamic-update-slice.1), channel_id=1, replica_groups=mesh['dp'=8,'grp'=4] {'dp','grp'}, use_global_device_ids=true, to_apply=%add.1 | all-reduce | flops 128 | bytes 1024
  43.5 41.1 %all-gather.4 = bf16[32,4,1024]{2,1,0:T(4,128)(2,1)S(1)} all-gather(bf16[1,4,1024]{2,1,0:T(4,128)(2,1)} %bitcast.56), channel_id=1, replica_groups=mesh['dp'=8,'grp'=4] {'dp','grp'}, dimensions={0}, use_global_device_ids=true | all-gather | bytes 270336 | tf_op jit(solution)/shard_map/all_gather | solution.py:94
  84.7 0.1 reshape.95
  84.7 1.0 fusion.49
  85.8 0.8 select_reduce_fusion
  86.6 0.2 dynamic-update-slice.3
  86.8 0.2 dynamic-update-slice
  87.0 0.8 fusion.23
  87.8 0.8 fusion.16
  88.7 0.1 fusion.22
  88.8 0.1 bitcast_dynamic-update-slice_fusion
  88.9 0.1 bitcast_dynamic-update-slice_fusion.1
  89.0 37.1 %all-reduce.5 = (f32[1024]{0:T(1024)S(1)}, f32[1024]{0:T(1024)S(1)}, f32[1024]{0:T(1024)S(1)}, f32[1024]{0:T(1024)S(1)}) all-reduce(f32[1024]{0:T(1024)S(1)} %dynamic-update-slice, f32[1024]{0:T(1024)S(1)} %bitcast_dynamic-update-slice_fusion.1, f32[1024]{0:T(1024)S(1)} %dynamic-update-slice.3, ...), channel_id=2, replica_groups=mesh['dp'=8,'grp'=4] {'dp','grp'}, use_global_device_ids=true, to_apply=%add | all-reduce | flops 4096 | bytes 32768
  126.1 0.1 reshape.75
  126.1 0.1 reshape.74
  126.2 0.1 reshape.73
  126.3 0.1 reshape.72
  126.3 1.6 %while.6 = (s32[]{:T(128)}, f32[32]{0:T(128)S(1)}, f32[32]{0:T(128)S(1)}, f32[32]{0:T(128)S(1)}, f32[32]{0:T(128)S(1)}, /*index=5*/f32[32,32]{1,0:T(8,128)S(1)},...) while((s32[]{:T(128)}, f32[32]{0:T(128)S(1)}, ...), condition=%wide.region_7.8_spmd, body=%wide.region_6.7_spmd.sunk | while | flops 389 | bytes 1691 | solution.py:17
  127.9 0.6 dynamic_slice.66
  128.5 0.1 fusion.20
  128.6 0.1 fusion.21
  128.8 0.5 convolution_add_fusion
  129.3 1.2 fusion.11
  (49 shorter events, 1.0 us)
Async XLA Ops:
  0.6 84.1 %copy-start = (bf16[256,1024]{1,0:T(8,128)(2,1)S(1)}, bf16[256,1024]{1,0:T(8,128)(2,1)}, u32[]{:S(2)}) copy-start(bf16[256,1024]{1,0:T(8,128)(2,1)} %param.6) | copy-start | bytes 1572868
  0.6 88.0 %copy-start.1 = (s32[256]{0:T(256)S(1)}, s32[256]{0:T(256)}, u32[]{:S(2)}) copy-start(s32[256]{0:T(256)} %param.8) | copy-start | bytes 3076
where the time goes:
time: 132 us; the launch traced here: 130 us
  blocking collectives  120 us (91%)
  other arithmetic  3.8 us (3%)
  matrix products  2.65 us (2%)
  local copies, waits for them, and re-layouts  2.51 us (2%)
    unnamed x2, blocking collectives  79 us
    all_gather x1, blocking collectives, shards(): lax.all_gather(captions, ('dp', 'grp'), axis=0, tiled=True)  41.1 us

commit v1 on v0

v1 whole, which is shorter than its diff:
```python
import math

import jax
import jax.numpy as jnp
from jax import lax
from jax.sharding import PartitionSpec as P

NEGATIVE = -1e30
AXES = ("dp", "grp")
ID_BASE = 256
ID_LANES = 128


def everywhere(block, devices):
    copies = jnp.broadcast_to(block[None], (devices,) + block.shape)
    return lax.all_to_all(copies, AXES, 0, 0)


def lookup(onehot, first_col, second_col):
    return jnp.dot(
        onehot, jnp.stack([first_col, second_col], axis=1), precision=lax.Precision.HIGHEST
    )


def group_totals(onehot, first_col, second_col):
    values = jnp.stack([first_col, second_col], axis=1)
    return lax.dot_general(
        onehot, values, (((0,), (0,)), ((), ())), precision=lax.Precision.HIGHEST
    )


def shards(clips, captions, clip_group, caption_group):
    clip_rows, feat_width = clips.shape
    devices = lax.axis_size("dp") * lax.axis_size("grp")
    groups = captions.shape[0] * devices // 4
    nclips_all = clip_rows * devices
    factor = 3.0 / math.sqrt(feat_width)

    digits = jnp.stack([caption_group // ID_BASE, caption_group % ID_BASE], axis=1)
    digits = jnp.pad(digits.astype(jnp.bfloat16), ((0, 0), (0, ID_LANES - 2)))
    packed = everywhere(jnp.concatenate([captions, digits], axis=1), devices)
    packed = packed.reshape(devices * captions.shape[0], feat_width + ID_LANES)
    caps = packed[:, :feat_width]
    ids = packed[:, feat_width : feat_width + 2].astype(jnp.int32)
    ids = ids[:, 0] * ID_BASE + ids[:, 1]

    scores = (
        lax.dot_general(clips, caps, (((1,), (1,)), ((), ())), preferred_element_type=jnp.float32)
        * factor
    )
    row_max = jnp.max(scores, axis=1)
    weights = jnp.exp(scores - row_max[:, None])
    row_sum = jnp.sum(weights, axis=1)
    positive = clip_group[:, None] == ids[None, :]
    masked = jnp.where(positive, scores, NEGATIVE)
    pos_max = jnp.max(masked, axis=1)
    pos_weights = jnp.where(positive, jnp.exp(masked - pos_max[:, None]), 0.0)
    pos_sum = jnp.sum(pos_weights, axis=1)
    all_part = jnp.dot(weights.astype(jnp.bfloat16), caps, preferred_element_type=jnp.float32)
    pos_part = jnp.dot(pos_weights.astype(jnp.bfloat16), caps, preferred_element_type=jnp.float32)

    member = clip_group[:, None] == jnp.arange(groups, dtype=jnp.int32)[None, :]
    onehot = member.astype(jnp.float32)
    local_top = jnp.max(jnp.where(member, row_max[:, None], NEGATIVE), axis=0)
    local_pos_top = jnp.max(jnp.where(member, pos_max[:, None], NEGATIVE), axis=0)
    picked_local = lookup(onehot, local_top, local_pos_top)
    local_lift = jnp.exp(row_max - picked_local[:, 0])
    local_pos_lift = jnp.exp(pos_max - picked_local[:, 1])
    group_sums = group_totals(onehot, local_lift * row_sum, local_pos_lift * pos_sum)

    stats = jnp.concatenate([local_top, group_sums[:, 0], local_pos_top, group_sums[:, 1]])
    stats = everywhere(stats.reshape(1, -1), devices).reshape(devices, 4, groups)
    top_all = jnp.max(stats[:, 0], axis=0)
    top_pos = jnp.max(stats[:, 2], axis=0)
    denominator = jnp.sum(stats[:, 1] * jnp.exp(stats[:, 0] - top_all[None]), axis=0)
    numerator = jnp.sum(stats[:, 3] * jnp.exp(stats[:, 2] - top_pos[None]), axis=0)

    picked = lookup(onehot, top_all, top_pos)
    factors = lookup(onehot, 1.0 / denominator, 1.0 / numerator)
    gain_all = jnp.exp(row_max - picked[:, 0]) * factors[:, 0]
    gain_pos = jnp.exp(pos_max - picked[:, 1]) * factors[:, 1]
    full_loss = top_all + jnp.log(denominator) - (top_pos + jnp.log(numerator))
    own_share = groups // lax.axis_size("grp")
    group_loss = lax.dynamic_slice_in_dim(full_loss, lax.axis_index("grp") * own_share, own_share)
    clip_grad = (nclips_all / groups) * (
        gain_all[:, None] * all_part - gain_pos[:, None] * pos_part
    )
    return (clip_grad, group_loss)


def solution(mesh):
    return jax.shard_map(
        shards,
        mesh=mesh,
        in_specs=(P(AXES, None), P(AXES, None), P(AXES), P(AXES)),
        out_specs=(P(AXES, None), P("grp")),
        check_vma=False,
    )
```

time: 132 us -> 36.7 us (0.28); the launches traced: 130 us -> 36.5 us
  blocking collectives: 120 us -> 18.5 us
  waiting for transfers between devices: 0 us -> 7.1 us
  starting transfers between devices: 0 us -> 2.54 us
  other arithmetic: 3.8 us -> 2.18 us
    unnamed x2 -> x0, blocking collectives: 79 us -> none
    all_gather x1 -> x0, blocking collectives: 41.1 us -> none  [shards(): lax.all_gather(captions, ('dp', 'grp'), axis=0, tiled=True)]
    all_to_all x0 -> x1, blocking collectives: none -> 18.5 us  [everywhere(): return lax.all_to_all(copies, AXES, 0, 0)]
    all_to_all x0 -> x1, waiting for transfers between devices: none -> 7.1 us  [everywhere(): return lax.all_to_all(copies, AXES, 0, 0)]
    all_to_all x0 -> x1, starting transfers between devices: none -> 2.54 us  [everywhere(): return lax.all_to_all(copies, AXES, 0, 0)]
  transfers between devices with their start and end apart: 0 -> 1, of which waited for: 0 -> 1; matrix products, arithmetic and copies ran while one was open for 0% -> 0% of each run, Pallas kernels for 0% -> 0%
where the time goes in v1:
time: 36.7 us; the launch traced here: 36.5 us
  blocking collectives  18.5 us (50%)
  waiting for transfers between devices  7.1 us (19%)
  local copies, waits for them, and re-layouts  2.82 us (8%)
  matrix products  2.54 us (7%)
  starting transfers between devices  2.54 us (7%)
  other arithmetic  2.18 us (6%)
  between operations  0.77 us (2%)
    all_to_all x1, blocking collectives, everywhere(): return lax.all_to_all(copies, AXES, 0, 0)  18.5 us
    all_to_all x1, waiting for transfers between devices, everywhere(): return lax.all_to_all(copies, AXES, 0, 0)  7.1 us
    all_to_all x1, starting transfers between devices, everywhere(): return lax.all_to_all(copies, AXES, 0, 0)  2.54 us
    dot_general x1, matrix products, shards(): jnp.dot(pos_weights.astype(jnp.bfloat16), caps, preferred_element_type=jn...  1.38 us
    unnamed x7, local copies, waits for them, and re-layouts  0.8 us
    another operation x2, other arithmetic, shards(): jnp.stack([caption_group // ID_BASE, caption_group % ID_BASE], axis=1)  0.74 us
  transfers between devices with their start and end apart: 1, of which 1 were waited for; matrix products, arithmetic and copies ran while one was open for 0% of the time, Pallas kernels for 0%

profile of v1, /device:TPU:0, one launch (start us, length us, event | category | flops | bytes accessed | tf_op | source)
XLA Modules:
  0.0 36.5 jit_solution(17193595327608317969)
XLA Ops:
  0.7 0.7 %convert_bitcast_fusion = (bf16[4,1]{0,1:T(2,128)(2,1)S(1)}, bf16[4,1]{0,1:T(2,128)(2,1)S(1)}) fusion(s32[4]{0:T(128)} %param.7), kind=kLoop, calls=%fused_computation.80 | loop fusion | flops 84 | bytes 32 | tf_op jit(solution)/shard_map/stack | solution.py:39
  1.4 0.1 copy.25
  1.5 0.1 broadcast_in_dim.48
  1.6 18.5 %all_to_all.10 = bf16[32,4,1152]{2,1,0:T(4,128)(2,1)S(1)} all-to-all(bf16[32,4,1152]{2,1,0:T(4,128)(2,1)S(1)} %broadcast_in_dim.48), channel_id=1, replica_groups=mesh['dp'=8,'grp'=4] {'dp','grp'}, dimensions={0} | all-to-all | bytes 589824 | tf_op jit(solution)/shard_map/all_to_all | solution.py:16
  20.2 0.2 fusion.13
  20.4 0.3 fusion.55
  20.8 0.7 %copy-done.1 = s32[256]{0:T(256)S(1)} copy-done((s32[256]{0:T(256)S(1)}, s32[256]{0:T(256)}, u32[]{:S(2)}) %copy-start.1) | copy-done | bytes 1048
  21.4 0.1 fusion.8
  21.5 0.1 select_reduce_fusion.1
  21.7 0.1 fusion.7
  21.8 0.1 fusion.23
  21.9 0.1 fusion.22
  22.1 0.1 pad_maximum_fusion.3
  22.1 0.6 %broadcast_in_dim.54 = f32[32,1,128]{2,1,0:T(1,128)} broadcast(f32[128]{0:T(128)S(1)} %pad_maximum_fusion.3), dimensions={2} | broadcast | bytes 16896 | tf_op jit(solution)/shard_map/broadcast_in_dim | solution.py:15
  22.8 2.5 %all-to-all-start.1 = ((f32[32,1,128]{2,1,0:T(1,128)}), f32[32,1,128]{2,1,0:T(1,128)S(1)}, u32[]{:S(2)}, u32[]{:S(2)}) async-start(f32[32,1,128]{2,1,0:T(1,128)} %broadcast_in_dim.54), calls=%async_computation.1 | async-start | bytes 32768 | tf_op jit(solution)/shard_map/all_to_all | solution.py:16
  25.3 7.1 %all-to-all-done.1 = f32[32,1,128]{2,1,0:T(1,128)S(1)} async-done(((f32[32,1,128]{2,1,0:T(1,128)}), f32[32,1,128]{2,1,0:T(1,128)S(1)}, u32[]{:S(2)}, u32[]{:S(2)}) %all-to-all-start.1) | async-done | bytes 16416 | tf_op jit(solution)/shard_map/all_to_all | solution.py:16
  32.4 0.5 %broadcast.77 = f32[]{:T(128)} broadcast(f32[]{:T(128)} %constant.124), dimensions={} | broadcast | bytes 8 | tf_op jit(solution)/shard_map/all_to_all | solution.py:16
  32.9 0.7 %reduce.8 = f32[32,128]{1,0:T(8,128)S(1)} reduce(f32[32,1,128]{2,1,0:T(1,128)S(1)} %all-to-all-done.1, f32[]{:T(128)} %broadcast.77), dimensions={1}, to_apply=%all_to_all.7.reduce_sub_computation.3 | reduce | bytes 32772 | tf_op jit(solution)/shard_map/all_to_all | solution.py:16
  33.6 0.1 reshape.57
  33.9 0.1 fusion.20
  34.0 0.1 fusion.21
  34.2 0.3 convolution_multiply_fusion.1
  34.5 0.6 %dynamic_slice.3 = f32[8]{0:T(128)} dynamic-slice(f32[32]{0:T(128)S(1)} %get-tuple-element.16, s32[]{:T(128)S(6)} %select_n.35), dynamic_slice_sizes={8} | dynamic-slice | bytes 68 | tf_op jit(solution)/shard_map/dynamic_slice | solution.py:84
  35.1 1.4 %fusion.1 = f32[256,1024]{1,0:T(8,128)} fusion(f32[256,1024]{1,0:T(8,128)S(1)} %convolution_multiply_fusion.1, f32[256]{0:T(256)S(1)} %bitcast.62, bf16[128,1152]{1,0:T(8,128)(2,1)S(1)} %reshape.56, f32[128,256]{1,0:T(8,128)S(1)} %get-tuple-element.22, f32[256]{0:T(256)S(1)} %fusion.8, s32[256]{0:T(256)S(1)} %copy-done.1, s32[128]{0:T(128)S(1)} %fusion.13), kind=kOutput, calls=%fused_computation.2 | convolution fusion | flops 68059136 | bytes 2493952 | tf_op jit(solution)/shard_map/dot_general | solution.py:60
  (17 shorter events, 0.3 us)
Async XLA Ops:
  0.6 19.8 %copy-start = (bf16[256,1024]{1,0:T(8,128)(2,1)S(1)}, bf16[256,1024]{1,0:T(8,128)(2,1)}, u32[]{:S(2)}) copy-start(bf16[256,1024]{1,0:T(8,128)(2,1)} %param.4) | copy-start | bytes 1572868
  0.6 0.9 %copy-start.2 = (bf16[4,1024]{1,0:T(4,128)(2,1)S(1)}, bf16[4,1024]{1,0:T(4,128)(2,1)}, u32[]{:S(2)}) copy-start(bf16[4,1024]{1,0:T(4,128)(2,1)} %param.5) | copy-start | bytes 24580
  20.8 0.7 %copy-start.1 = (s32[256]{0:T(256)S(1)}, s32[256]{0:T(256)}, u32[]{:S(2)}) copy-start(s32[256]{0:T(256)} %param.6) | copy-start | bytes 3076
  22.8 9.7 %all-to-all-start.1 = ((f32[32,1,128]{2,1,0:T(1,128)}), f32[32,1,128]{2,1,0:T(1,128)S(1)}, u32[]{:S(2)}, u32[]{:S(2)}) async-start(f32[32,1,128]{2,1,0:T(1,128)} %broadcast_in_dim.54), calls=%async_computation.1 | async-start | bytes 32768 | tf_op jit(solution)/shard_map/all_to_all | solution.py:16

commit v2 on v1

v2 whole, which is shorter than its diff:
```python
import functools
import math

import jax
import jax.numpy as jnp
from jax import lax
from jax.experimental import pallas as pl
from jax.experimental.pallas import tpu as pltpu
from jax.sharding import PartitionSpec as P

NEGATIVE = -1e30
AXES = ("dp", "grp")
ID_BASE = 256
LANES = 128
VMEM = pl.BlockSpec(memory_space=pltpu.VMEM)


def score_kernel(
    factor, groups, clips_ref, mine_ref, other_ref, group_ref, stats_ref, lift_ref, all_ref, pos_ref, caps
):
    rows, width = clips_ref.shape
    half = mine_ref.shape[0]
    caps[:half, :] = mine_ref[...]
    caps[half:, :] = other_ref[...]

    weigh_digit = lax.broadcasted_iota(jnp.int32, (8, LANES), 1)
    weigh_digit = jnp.where(weigh_digit == 0, float(ID_BASE), jnp.where(weigh_digit == 1, 1.0, 0.0))
    ids = lax.dot_general(
        weigh_digit.astype(jnp.bfloat16),
        caps[:, width:],
        (((1,), (1,)), ((), ())),
        preferred_element_type=jnp.float32,
    )[:1, :]

    eye = lax.broadcasted_iota(jnp.int32, (LANES, LANES), 0) == lax.broadcasted_iota(
        jnp.int32, (LANES, LANES), 1
    )
    group_row = group_ref[...].astype(jnp.float32)
    group_col = jnp.concatenate(
        [
            jnp.sum(
                jnp.where(eye, group_row[:, start : start + LANES], 0.0), axis=1, keepdims=True
            )
            for start in range(0, rows, LANES)
        ],
        axis=0,
    )

    caps_now = caps[:, :width]
    scores = (
        lax.dot_general(
            clips_ref[...], caps_now, (((1,), (1,)), ((), ())), preferred_element_type=jnp.float32
        )
        * factor
    )
    positive = group_col == ids
    row_max = jnp.max(scores, axis=1, keepdims=True)
    weights = jnp.exp(scores - row_max)
    row_sum = jnp.sum(weights, axis=1, keepdims=True)
    masked = jnp.where(positive, scores, NEGATIVE)
    pos_max = jnp.max(masked, axis=1, keepdims=True)
    pos_weights = jnp.where(positive, jnp.exp(masked - pos_max), 0.0)
    pos_sum = jnp.sum(pos_weights, axis=1, keepdims=True)

    lane = lax.broadcasted_iota(jnp.int32, (1, 4 * groups), 1)
    member = group_col.astype(jnp.int32) == lax.rem(lane, groups)
    block = lane // groups
    is_all = block < 2
    tops = jnp.where(is_all, row_max, pos_max)
    local_top = jnp.max(jnp.where(member, tops, NEGATIVE), axis=0, keepdims=True)
    lifts = jnp.where(member, jnp.exp(jnp.where(member, tops - local_top, 0.0)), 0.0)
    sums = jnp.sum(lifts * jnp.where(is_all, row_sum, pos_sum), axis=0, keepdims=True)
    is_top = lax.rem(block, 2) == 0
    stats_ref[...] = jnp.broadcast_to(jnp.where(is_top, local_top, sums), stats_ref.shape)
    lift_ref[...] = jnp.where(is_top, lifts, 0.0)

    all_ref[...] = jnp.dot(
        weights.astype(jnp.bfloat16), caps_now, preferred_element_type=jnp.float32
    )
    pos_ref[...] = jnp.dot(
        pos_weights.astype(jnp.bfloat16), caps_now, preferred_element_type=jnp.float32
    )


def finish_kernel(
    scale, groups, chunk, stats_ref, local_ref, lift_ref, all_ref, pos_ref, grad_ref, loss_ref, out, sems
):
    lanes = 4 * groups
    stats = stats_ref[...]
    top = jnp.max(stats, axis=0, keepdims=True)
    lifted = stats * pltpu.roll(jnp.exp(stats - top), groups, 1)
    totals = jnp.broadcast_to(jnp.sum(lifted, axis=0, keepdims=True), (8, lanes))
    top = jnp.broadcast_to(top, (8, lanes))
    lane = lax.broadcasted_iota(jnp.int32, (8, lanes), 1)
    is_top = lax.rem(lane // groups, 2) == 0
    totals = jnp.where(is_top, pltpu.roll(totals, lanes - groups, 1), 1.0)
    local_top = jnp.broadcast_to(local_ref[:1, :], (8, lanes))
    gains = jnp.where(is_top, jnp.exp(local_top - top) / totals * scale, 0.0)[:1, :]
    is_all = lane[:1, :] < 2 * groups
    gains_all = jnp.where(is_all, gains, 0.0)
    gains_pos = jnp.where(is_all, 0.0, gains)

    rows = all_ref.shape[0]
    copies = []
    for index, start in enumerate(range(0, rows, chunk)):
        part = slice(start, start + chunk)
        lifts = lift_ref[part, :]
        gain_all = jnp.sum(lifts * gains_all, axis=1, keepdims=True)
        gain_pos = jnp.sum(lifts * gains_pos, axis=1, keepdims=True)
        out[part, :] = gain_all * all_ref[part, :] - gain_pos * pos_ref[part, :]
        copy = pltpu.make_async_copy(out.at[part, :], grad_ref.at[part, :], sems.at[index])
        copy.start()
        copies.append(copy)

    level = top + jnp.log(totals)
    loss = level - pltpu.roll(level, lanes - 2 * groups, 1)
    share = loss_ref.shape[1]
    offset = lax.axis_index("grp") * share
    loss_ref[...] = pltpu.roll(loss, lax.rem(lanes - offset, lanes), 1)[:1, :share]
    for copy in copies:
        copy.wait()


def shards(clips, captions, clip_group, caption_group):
    rows, width = clips.shape
    own_caps = captions.shape[0]
    grp = lax.axis_size("grp")
    devices = lax.axis_size("dp") * grp
    groups = own_caps * devices // 4
    factor = 3.0 / math.sqrt(width)

    digits = jnp.stack([caption_group // ID_BASE, caption_group % ID_BASE], axis=1)
    digits = jnp.pad(digits.astype(jnp.bfloat16), ((0, 0), (0, LANES - 2)))
    packed = jnp.concatenate([captions, digits], axis=1)
    halves = packed.reshape(2, own_caps // 2, width + LANES)
    halves = jnp.broadcast_to(halves[None], (devices // 2,) + halves.shape)
    halves = halves.reshape(devices, own_caps // 2, width + LANES)
    mine = lax.all_to_all(halves, AXES, 0, 0).reshape(-1, width + LANES)
    other = lax.ppermute(mine, "grp", [(i, i ^ 1) for i in range(grp)])

    grant = (6 << 20) + 24 * rows * own_caps * devices
    f32 = functools.partial(jax.ShapeDtypeStruct, dtype=jnp.float32)
    local, lifts, all_part, pos_part = pl.pallas_call(
        functools.partial(score_kernel, factor, groups),
        out_shape=[
            f32((devices, 4 * groups)),
            f32((rows, 4 * groups)),
            f32((rows, width)),
            f32((rows, width)),
        ],
        in_specs=[VMEM] * 4,
        out_specs=[VMEM] * 4,
        scratch_shapes=[pltpu.VMEM((own_caps * devices, width + LANES), jnp.bfloat16)],
        compiler_params=pltpu.CompilerParams(vmem_limit_bytes=grant),
        name="scores",
    )(clips, mine, other, clip_group.reshape(1, rows))

    stats = lax.all_to_all(local, AXES, 0, 0, tiled=True)

    chunk = rows // 8
    clip_grad, group_loss = pl.pallas_call(
        functools.partial(finish_kernel, rows * devices / groups, groups, chunk),
        out_shape=[f32((rows, width)), f32((1, groups // grp))],
        in_specs=[VMEM] * 5,
        out_specs=[pl.BlockSpec(memory_space=pl.ANY), VMEM],
        scratch_shapes=[
            pltpu.VMEM((rows, width), jnp.float32),
            pltpu.SemaphoreType.DMA((rows // chunk,)),
        ],
        compiler_params=pltpu.CompilerParams(vmem_limit_bytes=grant),
        name="finish",
    )(stats, local, lifts, all_part, pos_part)
    return (clip_grad, group_loss.reshape(-1))


def solution(mesh):
    return jax.shard_map(
        shards,
        mesh=mesh,
        in_specs=(P(AXES, None), P(AXES, None), P(AXES), P(AXES)),
        out_specs=(P(AXES, None), P("grp")),
        check_vma=False,
    )
```

time: 36.7 us -> 30.9 us (0.84)
  blocking collectives: 18.5 us -> 24.6 us
  waiting for transfers between devices: 7.1 us -> 1.11 us
  Pallas kernels: 0 us -> 2.98 us
  matrix products: 2.54 us -> 0 us
  local copies, waits for them, and re-layouts: 2.82 us -> 0.29 us
  starting transfers between devices: 2.54 us -> 0.33 us
  other arithmetic: 2.18 us -> 0.75 us
    all_to_all x1 -> x0, waiting for transfers between devices: 7.1 us -> none  [everywhere(): return lax.all_to_all(copies, AXES, 0, 0)]
    all_to_all x1 -> x2, blocking collectives: 18.5 us -> 24.6 us  [the longest x1 15.5 us: shards(): mine = lax.all_to_all(halves, AXES, 0, 0).reshape(-1, width + LANES)]
    pallas_call x0 -> x2, Pallas kernels: none -> 2.98 us  [the longest x1 1.81 us: shards(): pl.pallas_call(functools.partial(finish_kernel, rows * devices / groups,...]
    all_to_all x1 -> x0, starting transfers between devices: 2.54 us -> none  [everywhere(): return lax.all_to_all(copies, AXES, 0, 0)]
    dot_general x7 -> x0, matrix products: 2.54 us -> none  [the longest x1 1.38 us: shards(): jnp.dot(pos_weights.astype(jnp.bfloat16), caps, preferred_element_type=jn...]
    ppermute x0 -> x1, waiting for transfers between devices: none -> 1.11 us  [shards(): other = lax.ppermute(mine, 'grp', [(i, i ^ 1) for i in range(grp)])]
    all_to_all x1 -> x0, other arithmetic: 0.68 us -> none  [everywhere(): return lax.all_to_all(copies, AXES, 0, 0)]
    unnamed x7, local copies, waits for them, and re-layouts: 0.8 us -> 0.12 us
where the time goes in v2:
time: 30.9 us; the launch traced here: 30.8 us
  blocking collectives  24.6 us (80%)
  Pallas kernels  2.98 us (10%)
  waiting for transfers between devices  1.11 us (4%)
  other arithmetic  0.75 us (2%)
  between operations  0.68 us (2%)
  starting transfers between devices  0.33 us (1%)
    all_to_all x1, blocking collectives, shards(): mine = lax.all_to_all(halves, AXES, 0, 0).reshape(-1, width + LANES)  15.5 us
    all_to_all x1, blocking collectives, shards(): stats = lax.all_to_all(local, AXES, 0, 0, tiled=True)  9.09 us
    pallas_call x1, Pallas kernels, shards(): pl.pallas_call(functools.partial(finish_kernel, rows * devices / groups,...  1.81 us
    pallas_call x1, Pallas kernels, shards(): pl.pallas_call(functools.partial(score_kernel, factor, groups), out_shape...  1.17 us
    ppermute x1, waiting for transfers between devices, shards(): other = lax.ppermute(mine, 'grp', [(i, i ^ 1) for i in range(grp)])  1.11 us
    another operation x2, other arithmetic, shards(): jnp.stack([caption_group // ID_BASE, caption_group % ID_BASE], axis=1)  0.74 us
  transfers between devices with their start and end apart: 1, of which 1 were waited for; matrix products, arithmetic and copies ran while one was open for 0% of the time, Pallas kernels for 0%

profile of v2, /device:TPU:0, one launch (start us, length us, event | category | flops | bytes accessed | tf_op | source)
XLA Modules:
  0.0 30.8 jit_solution(6384477628393827636)
XLA Ops:
  0.6 0.0 copy-start.2
  0.6 0.0 copy-start
  0.6 0.7 %convert_bitcast_fusion = (bf16[4,1]{0,1:T(2,128)(2,1)S(1)}, bf16[4,1]{0,1:T(2,128)(2,1)S(1)}) fusion(s32[4]{0:T(128)} %param.7), kind=kLoop, calls=%fused_computation.11 | loop fusion | flops 84 | bytes 32 | tf_op jit(solution)/shard_map/stack | solution.py:132
  1.4 0.1 copy.9
  1.5 0.0 copy-done.2
  1.5 0.1 broadcast_in_dim.8
  1.6 15.5 %all_to_all.16 = bf16[32,2,1152]{2,1,0:T(2,128)(2,1)S(1)} all-to-all(bf16[32,2,1152]{2,1,0:T(2,128)(2,1)S(1)} %bitcast.14), channel_id=1, replica_groups=mesh['dp'=8,'grp'=4] {'dp','grp'}, dimensions={0} | all-to-all | bytes 294912 | tf_op jit(solution)/shard_map/all_to_all | solution.py:138
  17.2 0.1 reshape.20.mine_ref
  17.2 0.0 copy-start.1
  17.2 0.3 %collective-permute-start = (bf16[64,1152]{1,0:T(8,128)(2,1)S(1)}, bf16[64,1152]{1,0:T(8,128)(2,1)S(1)}, u32[]{:S(2)}, u32[]{:S(2)}) collective-permute-start(bf16[64,1152]{1,0:T(8,128)(2,1)S(1)} %reshape.20.mine_ref), channel_id=1, source_target_pairs={{0,1},{1,0},{2,3},{3,2},{4,5},{5,4},{6,7},{7,6},{8,9},{9,8},{10,11... | collective-permute-start | bytes 442376 | tf_op jit(solution)/shard_map/ppermute | solution.py:139
  17.6 1.1 %collective-permute-done.other_ref = bf16[64,1152]{1,0:T(8,128)(2,1)S(1)} collective-permute-done((bf16[64,1152]{1,0:T(8,128)(2,1)S(1)}, bf16[64,1152]{1,0:T(8,128)(2,1)S(1)}, u32[]{:S(2)}, u32[]{:S(2)}) %collective-permute-start) | collective-permute-done | bytes 147488 | tf_op jit(solution)/shard_map/ppermute | solution.py:139
  18.7 0.0 copy-done
  18.7 0.0 copy-done.1
  18.7 1.2 %scores.1 = (f32[32,128]{1,0:T(8,128)S(1)}, f32[256,128]{1,0:T(8,128)S(1)}, f32[256,1024]{1,0:T(8,128)S(1)}, f32[256,1024]{1,0:T(8,128)S(1)}) custom-call(bf16[256,1024]{1,0:T(8,128)(2,1)S(1)} %copy-done, bf16[64,1152]{1,0:T(8,128)(2,1)S(1)} %reshape.20.mine_ref, bf16[64,1152]{1,0:T(8,128)(2,1)S(1)} %collective-permute-done.other_ref, s32[1,256]{1,0:T(1,128)S(1)} %bitcast.13), custom_call_target="tpu_custom_call" | custom-call | tf_op jit(solution)/shard_map/scores/pallas_call | solution.py:143
  19.9 9.1 %all_to_all.17 = f32[32,1,128]{2,1,0:T(1,128)S(1)} all-to-all(f32[32,1,128]{2,1,0:T(1,128)S(1)} %bitcast.11), channel_id=1, replica_groups=mesh['dp'=8,'grp'=4] {'dp','grp'}, dimensions={0} | all-to-all | bytes 32768 | tf_op jit(solution)/shard_map/all_to_all | solution.py:158
  28.9 1.8 %finish.1 = (f32[256,1024]{1,0:T(8,128)}, f32[1,8]{1,0:T(1,128)}) custom-call(f32[32,128]{1,0:T(8,128)S(1)} %bitcast.12, f32[32,128]{1,0:T(8,128)S(1)} %get-tuple-element.8.local_ref, f32[256,128]{1,0:T(8,128)S(1)} %get-tuple-element.9.lift_ref, f32[256,1024]{1,0:T(8,128)S(1)} %get-tuple-element.10.all_ref, f32[256,1024]{1,0:T(8,128)S(1)} %get-tuple-element.11.pos_ref), custom_call_target="tpu_custom_call" | custom-call | tf_op jit(solution)/shard_map/finish/pallas_call | solution.py:161
  (3 shorter events, 0.0 us)
Async XLA Ops:
  0.6 0.9 %copy-start.2 = (bf16[4,1024]{1,0:T(4,128)(2,1)S(1)}, bf16[4,1024]{1,0:T(4,128)(2,1)}, u32[]{:S(2)}) copy-start(bf16[4,1024]{1,0:T(4,128)(2,1)} %param.5) | copy-start | bytes 24580
  0.6 18.0 %copy-start = (bf16[256,1024]{1,0:T(8,128)(2,1)S(1)}, bf16[256,1024]{1,0:T(8,128)(2,1)}, u32[]{:S(2)}) copy-start(bf16[256,1024]{1,0:T(8,128)(2,1)} %clips_ref.1) | copy-start | bytes 1572868
  17.2 1.5 %copy-start.1 = (s32[256]{0:T(256)S(1)}, s32[256]{0:T(256)}, u32[]{:S(2)}) copy-start(s32[256]{0:T(256)} %param.6) | copy-start | bytes 3076
  17.2 1.4 %collective-permute-start = (bf16[64,1152]{1,0:T(8,128)(2,1)S(1)}, bf16[64,1152]{1,0:T(8,128)(2,1)S(1)}, u32[]{:S(2)}, u32[]{:S(2)}) collective-permute-start(bf16[64,1152]{1,0:T(8,128)(2,1)S(1)} %reshape.20.mine_ref), channel_id=1, source_target_pairs={{0,1},{1,0},{2,3},{3,2},{4,5},{5,4},{6,7},{7,6},{8,9},{9,8},{10,11... | collective-permute-start | bytes 442376 | tf_op jit(solution)/shard_map/ppermute | solution.py:139

commit v3 on v2

--- a/solution.py
+++ b/solution.py
@@ -10,9 +10,11 @@
 
 NEGATIVE = -1e30
 AXES = ("dp", "grp")
-ID_BASE = 256
+ID_BITS = 8
+ID_BASE = 1 << ID_BITS
 LANES = 128
 VMEM = pl.BlockSpec(memory_space=pltpu.VMEM)
+HBM = pl.BlockSpec(memory_space=pltpu.HBM)
 
 
 def score_kernel(
@@ -82,8 +84,46 @@
     )
 
 
+def pack_kernel(ids_ref, caps_ref, packed_ref, caps, ids, sems):
+    copies = [
+        pltpu.make_async_copy(ids_ref, ids, sems.at[0]),
+        pltpu.make_async_copy(caps_ref, caps, sems.at[1]),
+    ]
+    for copy in copies:
+        copy.start()
+    for copy in copies:
+        copy.wait()
+    own_caps, width = caps.shape
+    half = own_caps // 2
+    row = lax.broadcasted_iota(jnp.int32, (own_caps, LANES), 0)
+    lane = lax.broadcasted_iota(jnp.int32, (own_caps, LANES), 1)
+    digits = jnp.zeros((own_caps, LANES), jnp.int32)
+    for index in range(own_caps):
+        high = lax.shift_right_logical(ids[index], ID_BITS)
+        low = jnp.bitwise_and(ids[index], ID_BASE - 1)
+        here = jnp.where(lane == 0, high, jnp.where(lane == 1, low, 0))
+        digits = jnp.where(row == index, here, digits)
+    digits = digits.astype(jnp.float32).astype(jnp.bfloat16)
+    for part in range(2):
+        packed_ref[part, :, :width] = caps[part * half : (part + 1) * half, :]
+        packed_ref[part, :, width:] = digits[part * half : (part + 1) * half, :]
+
+
 def finish_kernel(
-    scale, groups, chunk, stats_ref, local_ref, lift_ref, all_ref, pos_ref, grad_ref, loss_ref, out, sems
+    scale,
+    groups,
+    chunk,
+    stats_ref,
+    local_ref,
+    lift_ref,
+    all_ref,
+    pos_ref,
+    grad_ref,
+    loss_ref,
+    out,
+    loss_out,
+    sems,
+    loss_sem,
 ):
     lanes = 4 * groups
     stats = stats_ref[...]
@@ -100,8 +140,16 @@
     gains_all = jnp.where(is_all, gains, 0.0)
     gains_pos = jnp.where(is_all, 0.0, gains)
 
+    level = top + jnp.log(totals)
+    loss = level - pltpu.roll(level, lanes - 2 * groups, 1)
+    share = loss_out.shape[1]
+    offset = lax.axis_index("grp") * share
+    loss_out[...] = pltpu.roll(loss, lax.rem(lanes - offset, lanes), 1)[:1, :share]
+    loss_copy = pltpu.make_async_copy(loss_out, loss_ref, loss_sem)
+    loss_copy.start()
+
     rows = all_ref.shape[0]
-    copies = []
+    copies = [loss_copy]
     for index, start in enumerate(range(0, rows, chunk)):
         part = slice(start, start + chunk)
         lifts = lift_ref[part, :]
@@ -112,11 +160,6 @@
         copy.start()
         copies.append(copy)
 
-    level = top + jnp.log(totals)
-    loss = level - pltpu.roll(level, lanes - 2 * groups, 1)
-    share = loss_ref.shape[1]
-    offset = lax.axis_index("grp") * share
-    loss_ref[...] = pltpu.roll(loss, lax.rem(lanes - offset, lanes), 1)[:1, :share]
     for copy in copies:
         copy.wait()
 
@@ -129,10 +172,19 @@
     groups = own_caps * devices // 4
     factor = 3.0 / math.sqrt(width)
 
-    digits = jnp.stack([caption_group // ID_BASE, caption_group % ID_BASE], axis=1)
-    digits = jnp.pad(digits.astype(jnp.bfloat16), ((0, 0), (0, LANES - 2)))
-    packed = jnp.concatenate([captions, digits], axis=1)
-    halves = packed.reshape(2, own_caps // 2, width + LANES)
+    halves = pl.pallas_call(
+        pack_kernel,
+        out_shape=jax.ShapeDtypeStruct((2, own_caps // 2, width + LANES), captions.dtype),
+        in_specs=[HBM] * 2,
+        out_specs=VMEM,
+        scratch_shapes=[
+            pltpu.VMEM(captions.shape, captions.dtype),
+            pltpu.SMEM(caption_group.shape, caption_group.dtype),
+            pltpu.SemaphoreType.DMA((2,)),
+        ],
+        compiler_params=pltpu.CompilerParams(vmem_limit_bytes=1 << 20),
+        name="pack",
+    )(*[pltpu.with_memory_space_constraint(a, pltpu.HBM) for a in (caption_group, captions)])
     halves = jnp.broadcast_to(halves[None], (devices // 2,) + halves.shape)
     halves = halves.reshape(devices, own_caps // 2, width + LANES)
     mine = lax.all_to_all(halves, AXES, 0, 0).reshape(-1, width + LANES)
@@ -162,10 +214,12 @@
         functools.partial(finish_kernel, rows * devices / groups, groups, chunk),
         out_shape=[f32((rows, width)), f32((1, groups // grp))],
         in_specs=[VMEM] * 5,
-        out_specs=[pl.BlockSpec(memory_space=pl.ANY), VMEM],
+        out_specs=[HBM, HBM],
         scratch_shapes=[
             pltpu.VMEM((rows, width), jnp.float32),
+            pltpu.VMEM((1, groups // grp), jnp.float32),
             pltpu.SemaphoreType.DMA((rows // chunk,)),
+            pltpu.SemaphoreType.DMA,
         ],
         compiler_params=pltpu.CompilerParams(vmem_limit_bytes=grant),
         name="finish",

time: 30.9 us -> 30.4 us (0.984)
  other arithmetic: 0.75 us -> 0 us
  Pallas kernels: 2.98 us -> 3.32 us
    pallas_call x0 -> x1, Pallas kernels: none -> 0.82 us  [shards(): pl.pallas_call(pack_kernel, out_shape=jax.ShapeDtypeStruct((2, own_caps /...]
    another operation x2 -> x0, other arithmetic: 0.74 us -> none  [shards(): jnp.stack([caption_group // ID_BASE, caption_group % ID_BASE], axis=1)]
    pallas_call x1, Pallas kernels: 1.81 us -> 1.32 us  [shards(): pl.pallas_call(functools.partial(finish_kernel, rows * devices / groups,...]
where the time goes in v3:
time: 30.4 us; the launch traced here: 30.2 us
  blocking collectives  24.6 us (81%)
  Pallas kernels  3.32 us (11%)
  waiting for transfers between devices  1.11 us (4%)
  between operations  0.67 us (2%)
  starting transfers between devices  0.33 us (1%)
    all_to_all x1, blocking collectives, shards(): mine = lax.all_to_all(halves, AXES, 0, 0).reshape(-1, width + LANES)  15.5 us
    all_to_all x1, blocking collectives, shards(): stats = lax.all_to_all(local, AXES, 0, 0, tiled=True)  9.08 us
    pallas_call x1, Pallas kernels, shards(): pl.pallas_call(functools.partial(finish_kernel, rows * devices / groups,...  1.32 us
    pallas_call x1, Pallas kernels, shards(): pl.pallas_call(functools.partial(score_kernel, factor, groups), out_shape...  1.17 us
    ppermute x1, waiting for transfers between devices, shards(): other = lax.ppermute(mine, 'grp', [(i, i ^ 1) for i in range(grp)])  1.11 us
    pallas_call x1, Pallas kernels, shards(): pl.pallas_call(pack_kernel, out_shape=jax.ShapeDtypeStruct((2, own_caps /...  0.82 us
  transfers between devices with their start and end apart: 1, of which 1 were waited for; matrix products, arithmetic and copies ran while one was open for 0% of the time, Pallas kernels for 0%

profile of v3, /device:TPU:0, one launch (start us, length us, event | category | flops | bytes accessed | tf_op | source)
XLA Modules:
  0.0 30.2 jit_solution(16796996405893119533)
XLA Ops:
  0.6 0.0 copy-start
  0.6 0.8 %pack.1 = bf16[2,2,1152]{2,1,0:T(2,128)(2,1)S(1)} custom-call(s32[4]{0:T(128)} %ids_ref.1, bf16[4,1024]{1,0:T(4,128)(2,1)} %caps_ref.1), custom_call_target="tpu_custom_call" | custom-call | tf_op jit(solution)/shard_map/pack/pallas_call | solution.py:175
  1.5 0.1 broadcast_in_dim.2
  1.6 15.5 %all_to_all.16 = bf16[32,2,1152]{2,1,0:T(2,128)(2,1)S(1)} all-to-all(bf16[32,2,1152]{2,1,0:T(2,128)(2,1)S(1)} %bitcast.10), channel_id=1, replica_groups=mesh['dp'=8,'grp'=4] {'dp','grp'}, dimensions={0} | all-to-all | bytes 294912 | tf_op jit(solution)/shard_map/all_to_all | solution.py:190
  17.1 0.1 reshape.20.mine_ref
  17.2 0.0 copy-start.1
  17.2 0.3 %collective-permute-start = (bf16[64,1152]{1,0:T(8,128)(2,1)S(1)}, bf16[64,1152]{1,0:T(8,128)(2,1)S(1)}, u32[]{:S(2)}, u32[]{:S(2)}) collective-permute-start(bf16[64,1152]{1,0:T(8,128)(2,1)S(1)} %reshape.20.mine_ref), channel_id=1, source_target_pairs={{0,1},{1,0},{2,3},{3,2},{4,5},{5,4},{6,7},{7,6},{8,9},{9,8},{10,11... | collective-permute-start | bytes 442376 | tf_op jit(solution)/shard_map/ppermute | solution.py:191
  17.5 1.1 %collective-permute-done.other_ref = bf16[64,1152]{1,0:T(8,128)(2,1)S(1)} collective-permute-done((bf16[64,1152]{1,0:T(8,128)(2,1)S(1)}, bf16[64,1152]{1,0:T(8,128)(2,1)S(1)}, u32[]{:S(2)}, u32[]{:S(2)}) %collective-permute-start) | collective-permute-done | bytes 147488 | tf_op jit(solution)/shard_map/ppermute | solution.py:191
  18.6 0.0 copy-done
  18.6 0.0 copy-done.1
  18.6 1.2 %scores.1 = (f32[32,128]{1,0:T(8,128)S(1)}, f32[256,128]{1,0:T(8,128)S(1)}, f32[256,1024]{1,0:T(8,128)S(1)}, f32[256,1024]{1,0:T(8,128)S(1)}) custom-call(bf16[256,1024]{1,0:T(8,128)(2,1)S(1)} %copy-done, bf16[64,1152]{1,0:T(8,128)(2,1)S(1)} %reshape.20.mine_ref, bf16[64,1152]{1,0:T(8,128)(2,1)S(1)} %collective-permute-done.other_ref, s32[1,256]{1,0:T(1,128)S(1)} %bitcast.9), custom_call_target="tpu_custom_call" | custom-call | tf_op jit(solution)/shard_map/scores/pallas_call | solution.py:195
  19.8 9.1 %all_to_all.17 = f32[32,1,128]{2,1,0:T(1,128)S(1)} all-to-all(f32[32,1,128]{2,1,0:T(1,128)S(1)} %bitcast.7), channel_id=1, replica_groups=mesh['dp'=8,'grp'=4] {'dp','grp'}, dimensions={0} | all-to-all | bytes 32768 | tf_op jit(solution)/shard_map/all_to_all | solution.py:210
  28.9 1.3 %finish.1 = (f32[256,1024]{1,0:T(8,128)}, f32[1,8]{1,0:T(1,128)}) custom-call(f32[32,128]{1,0:T(8,128)S(1)} %bitcast.8, f32[32,128]{1,0:T(8,128)S(1)} %get-tuple-element.8.local_ref, f32[256,128]{1,0:T(8,128)S(1)} %get-tuple-element.9.lift_ref, f32[256,1024]{1,0:T(8,128)S(1)} %get-tuple-element.10.all_ref, f32[256,1024]{1,0:T(8,128)S(1)} %get-tuple-element.11.pos_ref), custom_call_target="tpu_custom_call" | custom-call | tf_op jit(solution)/shard_map/finish/pallas_call | solution.py:213
Async XLA Ops:
  0.6 18.0 %copy-start = (bf16[256,1024]{1,0:T(8,128)(2,1)S(1)}, bf16[256,1024]{1,0:T(8,128)(2,1)}, u32[]{:S(2)}) copy-start(bf16[256,1024]{1,0:T(8,128)(2,1)} %clips_ref.1) | copy-start | bytes 1572868
  17.2 1.5 %copy-start.1 = (s32[256]{0:T(256)S(1)}, s32[256]{0:T(256)}, u32[]{:S(2)}) copy-start(s32[256]{0:T(256)} %param.6) | copy-start | bytes 3076
  17.2 1.4 %collective-permute-start = (bf16[64,1152]{1,0:T(8,128)(2,1)S(1)}, bf16[64,1152]{1,0:T(8,128)(2,1)S(1)}, u32[]{:S(2)}, u32[]{:S(2)}) collective-permute-start(bf16[64,1152]{1,0:T(8,128)(2,1)S(1)} %reshape.20.mine_ref), channel_id=1, source_target_pairs={{0,1},{1,0},{2,3},{3,2},{4,5},{5,4},{6,7},{7,6},{8,9},{9,8},{10,11... | collective-permute-start | bytes 442376 | tf_op jit(solution)/shard_map/ppermute | solution.py:191

commit v4 on v3

--- a/solution.py
+++ b/solution.py
@@ -13,6 +13,7 @@
 ID_BITS = 8
 ID_BASE = 1 << ID_BITS
 LANES = 128
+ROW_CHUNK = 128
 VMEM = pl.BlockSpec(memory_space=pltpu.VMEM)
 HBM = pl.BlockSpec(memory_space=pltpu.HBM)
 
@@ -49,39 +50,53 @@
     )
 
     caps_now = caps[:, :width]
-    scores = (
-        lax.dot_general(
-            clips_ref[...], caps_now, (((1,), (1,)), ((), ())), preferred_element_type=jnp.float32
-        )
-        * factor
-    )
-    positive = group_col == ids
-    row_max = jnp.max(scores, axis=1, keepdims=True)
-    weights = jnp.exp(scores - row_max)
-    row_sum = jnp.sum(weights, axis=1, keepdims=True)
-    masked = jnp.where(positive, scores, NEGATIVE)
-    pos_max = jnp.max(masked, axis=1, keepdims=True)
-    pos_weights = jnp.where(positive, jnp.exp(masked - pos_max), 0.0)
-    pos_sum = jnp.sum(pos_weights, axis=1, keepdims=True)
-
     lane = lax.broadcasted_iota(jnp.int32, (1, 4 * groups), 1)
-    member = group_col.astype(jnp.int32) == lax.rem(lane, groups)
     block = lane // groups
     is_all = block < 2
-    tops = jnp.where(is_all, row_max, pos_max)
-    local_top = jnp.max(jnp.where(member, tops, NEGATIVE), axis=0, keepdims=True)
-    lifts = jnp.where(member, jnp.exp(jnp.where(member, tops - local_top, 0.0)), 0.0)
-    sums = jnp.sum(lifts * jnp.where(is_all, row_sum, pos_sum), axis=0, keepdims=True)
     is_top = lax.rem(block, 2) == 0
+    lane_group = lax.rem(lane, groups).astype(jnp.float32)
+
+    parts = [slice(start, start + ROW_CHUNK) for start in range(0, rows, ROW_CHUNK)]
+    top_list, total_list, member_list, weight_list = [], [], [], []
+    local_top = None
+
+    for part in parts:
+        group_part = group_col[part]
+        scores = (
+            lax.dot_general(
+                clips_ref[part, :],
+                caps_now,
+                (((1,), (1,)), ((), ())),
+                preferred_element_type=jnp.float32,
+            )
+            * factor
+        )
+        positive = group_part == ids
+        masked = jnp.where(positive, scores, NEGATIVE)
+        row_max = jnp.max(scores, axis=1, keepdims=True)
+        pos_max = jnp.max(masked, axis=1, keepdims=True)
+        weights = jnp.exp(scores - row_max)
+        pos_weights = jnp.exp(masked - pos_max)
+        weight_list.append((weights.astype(jnp.bfloat16), pos_weights.astype(jnp.bfloat16)))
+        row_sum = jnp.sum(weights, axis=1, keepdims=True)
+        pos_sum = jnp.sum(pos_weights, axis=1, keepdims=True)
+        member = group_part == lane_group
+        top = jnp.where(member, jnp.where(is_all, row_max, pos_max), NEGATIVE)
+        here = jnp.max(top, axis=0, keepdims=True)
+        local_top = here if local_top is None else jnp.maximum(local_top, here)
+        top_list.append(top)
+        total_list.append((row_sum, pos_sum))
+        member_list.append(member)
+    for kind, ref in enumerate((all_ref, pos_ref)):
+        for part, pair in zip(parts, weight_list):
+            ref[part, :] = jnp.dot(pair[kind], caps_now, preferred_element_type=jnp.float32)
+    sums = 0.0
+    for index, part in enumerate(parts):
+        lifts = jnp.where(member_list[index], jnp.exp(top_list[index] - local_top), 0.0)
+        row_sum, pos_sum = total_list[index]
+        sums = sums + jnp.sum(lifts * jnp.where(is_all, row_sum, pos_sum), axis=0, keepdims=True)
+        lift_ref[part, :] = jnp.where(is_top, lifts, 0.0)
     stats_ref[...] = jnp.broadcast_to(jnp.where(is_top, local_top, sums), stats_ref.shape)
-    lift_ref[...] = jnp.where(is_top, lifts, 0.0)
-
-    all_ref[...] = jnp.dot(
-        weights.astype(jnp.bfloat16), caps_now, preferred_element_type=jnp.float32
-    )
-    pos_ref[...] = jnp.dot(
-        pos_weights.astype(jnp.bfloat16), caps_now, preferred_element_type=jnp.float32
-    )
 
 
 def pack_kernel(ids_ref, caps_ref, packed_ref, caps, ids, sems):
@@ -140,16 +155,8 @@
     gains_all = jnp.where(is_all, gains, 0.0)
     gains_pos = jnp.where(is_all, 0.0, gains)
 
-    level = top + jnp.log(totals)
-    loss = level - pltpu.roll(level, lanes - 2 * groups, 1)
-    share = loss_out.shape[1]
-    offset = lax.axis_index("grp") * share
-    loss_out[...] = pltpu.roll(loss, lax.rem(lanes - offset, lanes), 1)[:1, :share]
-    loss_copy = pltpu.make_async_copy(loss_out, loss_ref, loss_sem)
-    loss_copy.start()
-
     rows = all_ref.shape[0]
-    copies = [loss_copy]
+    copies = []
     for index, start in enumerate(range(0, rows, chunk)):
         part = slice(start, start + chunk)
         lifts = lift_ref[part, :]
@@ -159,6 +166,15 @@
         copy = pltpu.make_async_copy(out.at[part, :], grad_ref.at[part, :], sems.at[index])
         copy.start()
         copies.append(copy)
+
+    level = top + jnp.log(totals)
+    loss = level - pltpu.roll(level, lanes - 2 * groups, 1)
+    share = loss_out.shape[1]
+    offset = lax.axis_index("grp") * share
+    loss_out[...] = pltpu.roll(loss, lax.rem(lanes - offset, lanes), 1)[:1, :share]
+    loss_copy = pltpu.make_async_copy(loss_out, loss_ref, loss_sem)
+    loss_copy.start()
+    copies.append(loss_copy)
 
     for copy in copies:
         copy.wait()

time: 30.4 us -> 30.1 us (level)
  no operation moved by 1% of the time
where the time goes in v4:
time: 30.1 us; the launch traced here: 29.9 us
  blocking collectives  24.6 us (82%)
  Pallas kernels  3.03 us (10%)
  waiting for transfers between devices  1.11 us (4%)
  between operations  0.67 us (2%)
  starting transfers between devices  0.33 us (1%)
    all_to_all x1, blocking collectives, shards(): mine = lax.all_to_all(halves, AXES, 0, 0).reshape(-1, width + LANES)  15.5 us
    all_to_all x1, blocking collectives, shards(): stats = lax.all_to_all(local, AXES, 0, 0, tiled=True)  9.09 us
    pallas_call x1, Pallas kernels, shards(): pl.pallas_call(functools.partial(finish_kernel, rows * devices / groups,...  1.31 us
    ppermute x1, waiting for transfers between devices, shards(): other = lax.ppermute(mine, 'grp', [(i, i ^ 1) for i in range(grp)])  1.11 us
    pallas_call x1, Pallas kernels, shards(): pl.pallas_call(functools.partial(score_kernel, factor, groups), out_shape...  0.89 us
    pallas_call x1, Pallas kernels, shards(): pl.pallas_call(pack_kernel, out_shape=jax.ShapeDtypeStruct((2, own_caps /...  0.82 us
  transfers between devices with their start and end apart: 1, of which 1 were waited for; matrix products, arithmetic and copies ran while one was open for 0% of the time, Pallas kernels for 0%

profile of v4, /device:TPU:0, one launch (start us, length us, event | category | flops | bytes accessed | tf_op | source)
XLA Modules:
  0.0 29.9 jit_solution(2960943699175359234)
XLA Ops:
  0.6 0.0 copy-start
  0.6 0.8 %pack.1 = bf16[2,2,1152]{2,1,0:T(2,128)(2,1)S(1)} custom-call(s32[4]{0:T(128)} %ids_ref.1, bf16[4,1024]{1,0:T(4,128)(2,1)} %caps_ref.1), custom_call_target="tpu_custom_call" | custom-call | tf_op jit(solution)/shard_map/pack/pallas_call | solution.py:191
  1.5 0.1 broadcast_in_dim.2
  1.6 15.5 %all_to_all.16 = bf16[32,2,1152]{2,1,0:T(2,128)(2,1)S(1)} all-to-all(bf16[32,2,1152]{2,1,0:T(2,128)(2,1)S(1)} %bitcast.10), channel_id=1, replica_groups=mesh['dp'=8,'grp'=4] {'dp','grp'}, dimensions={0} | all-to-all | bytes 294912 | tf_op jit(solution)/shard_map/all_to_all | solution.py:206
  17.1 0.1 reshape.20.mine_ref
  17.2 0.0 copy-start.1
  17.2 0.3 %collective-permute-start = (bf16[64,1152]{1,0:T(8,128)(2,1)S(1)}, bf16[64,1152]{1,0:T(8,128)(2,1)S(1)}, u32[]{:S(2)}, u32[]{:S(2)}) collective-permute-start(bf16[64,1152]{1,0:T(8,128)(2,1)S(1)} %reshape.20.mine_ref), channel_id=1, source_target_pairs={{0,1},{1,0},{2,3},{3,2},{4,5},{5,4},{6,7},{7,6},{8,9},{9,8},{10,11... | collective-permute-start | bytes 442376 | tf_op jit(solution)/shard_map/ppermute | solution.py:207
  17.5 1.1 %collective-permute-done.other_ref = bf16[64,1152]{1,0:T(8,128)(2,1)S(1)} collective-permute-done((bf16[64,1152]{1,0:T(8,128)(2,1)S(1)}, bf16[64,1152]{1,0:T(8,128)(2,1)S(1)}, u32[]{:S(2)}, u32[]{:S(2)}) %collective-permute-start) | collective-permute-done | bytes 147488 | tf_op jit(solution)/shard_map/ppermute | solution.py:207
  18.6 0.0 copy-done
  18.6 0.0 copy-done.1
  18.6 0.9 %scores.1 = (f32[32,128]{1,0:T(8,128)S(1)}, f32[256,128]{1,0:T(8,128)S(1)}, f32[256,1024]{1,0:T(8,128)S(1)}, f32[256,1024]{1,0:T(8,128)S(1)}) custom-call(bf16[256,1024]{1,0:T(8,128)(2,1)S(1)} %copy-done, bf16[64,1152]{1,0:T(8,128)(2,1)S(1)} %reshape.20.mine_ref, bf16[64,1152]{1,0:T(8,128)(2,1)S(1)} %collective-permute-done.other_ref, s32[1,256]{1,0:T(1,128)S(1)} %bitcast.9), custom_call_target="tpu_custom_call" | custom-call | tf_op jit(solution)/shard_map/scores/pallas_call | solution.py:211
  19.5 9.1 %all_to_all.17 = f32[32,1,128]{2,1,0:T(1,128)S(1)} all-to-all(f32[32,1,128]{2,1,0:T(1,128)S(1)} %bitcast.7), channel_id=1, replica_groups=mesh['dp'=8,'grp'=4] {'dp','grp'}, dimensions={0} | all-to-all | bytes 32768 | tf_op jit(solution)/shard_map/all_to_all | solution.py:226
  28.6 1.3 %finish.1 = (f32[256,1024]{1,0:T(8,128)}, f32[1,8]{1,0:T(1,128)}) custom-call(f32[32,128]{1,0:T(8,128)S(1)} %bitcast.8, f32[32,128]{1,0:T(8,128)S(1)} %get-tuple-element.8.local_ref, f32[256,128]{1,0:T(8,128)S(1)} %get-tuple-element.9.lift_ref, f32[256,1024]{1,0:T(8,128)S(1)} %get-tuple-element.10.all_ref, f32[256,1024]{1,0:T(8,128)S(1)} %get-tuple-element.11.pos_ref), custom_call_target="tpu_custom_call" | custom-call | tf_op jit(solution)/shard_map/finish/pallas_call | solution.py:229
Async XLA Ops:
  0.6 18.0 %copy-start = (bf16[256,1024]{1,0:T(8,128)(2,1)S(1)}, bf16[256,1024]{1,0:T(8,128)(2,1)}, u32[]{:S(2)}) copy-start(bf16[256,1024]{1,0:T(8,128)(2,1)} %clips_ref.1) | copy-start | bytes 1572868
  17.2 1.5 %copy-start.1 = (s32[256]{0:T(256)S(1)}, s32[256]{0:T(256)}, u32[]{:S(2)}) copy-start(s32[256]{0:T(256)} %param.6) | copy-start | bytes 3076
  17.2 1.4 %collective-permute-start = (bf16[64,1152]{1,0:T(8,128)(2,1)S(1)}, bf16[64,1152]{1,0:T(8,128)(2,1)S(1)}, u32[]{:S(2)}, u32[]{:S(2)}) collective-permute-start(bf16[64,1152]{1,0:T(8,128)(2,1)S(1)} %reshape.20.mine_ref), channel_id=1, source_target_pairs={{0,1},{1,0},{2,3},{3,2},{4,5},{5,4},{6,7},{7,6},{8,9},{9,8},{10,11... | collective-permute-start | bytes 442376 | tf_op jit(solution)/shard_map/ppermute | solution.py:207

commit v5 on v4

--- a/solution.py
+++ b/solution.py
@@ -95,7 +95,7 @@
         lifts = jnp.where(member_list[index], jnp.exp(top_list[index] - local_top), 0.0)
         row_sum, pos_sum = total_list[index]
         sums = sums + jnp.sum(lifts * jnp.where(is_all, row_sum, pos_sum), axis=0, keepdims=True)
-        lift_ref[part, :] = jnp.where(is_top, lifts, 0.0)
+        lift_ref[part, :] = jnp.where(is_top, 0.0, lifts)
     stats_ref[...] = jnp.broadcast_to(jnp.where(is_top, local_top, sums), stats_ref.shape)
 
 
@@ -141,17 +141,17 @@
     loss_sem,
 ):
     lanes = 4 * groups
+    devices = stats_ref.shape[0]
     stats = stats_ref[...]
     top = jnp.max(stats, axis=0, keepdims=True)
-    lifted = stats * pltpu.roll(jnp.exp(stats - top), groups, 1)
-    totals = jnp.broadcast_to(jnp.sum(lifted, axis=0, keepdims=True), (8, lanes))
-    top = jnp.broadcast_to(top, (8, lanes))
-    lane = lax.broadcasted_iota(jnp.int32, (8, lanes), 1)
-    is_top = lax.rem(lane // groups, 2) == 0
-    totals = jnp.where(is_top, pltpu.roll(totals, lanes - groups, 1), 1.0)
-    local_top = jnp.broadcast_to(local_ref[:1, :], (8, lanes))
-    gains = jnp.where(is_top, jnp.exp(local_top - top) / totals * scale, 0.0)[:1, :]
-    is_all = lane[:1, :] < 2 * groups
+    lifts = jnp.exp(jnp.concatenate([stats, local_ref[:8, :]], axis=0) - top)
+    lifts = pltpu.roll(lifts, groups, 1)
+    totals = jnp.sum(stats * lifts[:devices], axis=0, keepdims=True)
+    lane = lax.broadcasted_iota(jnp.int32, (1, lanes), 1)
+    is_sum = lax.rem(lane // groups, 2) == 1
+    totals = jnp.where(is_sum, totals, 1.0)
+    gains = jnp.where(is_sum, lifts[devices : devices + 1] * (scale / totals), 0.0)
+    is_all = lane < 2 * groups
     gains_all = jnp.where(is_all, gains, 0.0)
     gains_pos = jnp.where(is_all, 0.0, gains)
 
@@ -159,19 +159,19 @@
     copies = []
     for index, start in enumerate(range(0, rows, chunk)):
         part = slice(start, start + chunk)
-        lifts = lift_ref[part, :]
-        gain_all = jnp.sum(lifts * gains_all, axis=1, keepdims=True)
-        gain_pos = jnp.sum(lifts * gains_pos, axis=1, keepdims=True)
+        own = lift_ref[part, :]
+        gain_all = jnp.sum(own * gains_all, axis=1, keepdims=True)
+        gain_pos = jnp.sum(own * gains_pos, axis=1, keepdims=True)
         out[part, :] = gain_all * all_ref[part, :] - gain_pos * pos_ref[part, :]
         copy = pltpu.make_async_copy(out.at[part, :], grad_ref.at[part, :], sems.at[index])
         copy.start()
         copies.append(copy)
 
-    level = top + jnp.log(totals)
+    level = pltpu.roll(jnp.broadcast_to(top, (8, lanes)), groups, 1) + jnp.log(totals)
     loss = level - pltpu.roll(level, lanes - 2 * groups, 1)
     share = loss_out.shape[1]
-    offset = lax.axis_index("grp") * share
-    loss_out[...] = pltpu.roll(loss, lax.rem(lanes - offset, lanes), 1)[:1, :share]
+    first = groups + lax.axis_index("grp") * share
+    loss_out[...] = pltpu.roll(loss, lanes - first, 1)[:1, :share]
     loss_copy = pltpu.make_async_copy(loss_out, loss_ref, loss_sem)
     loss_copy.start()
     copies.append(loss_copy)

time: 30.1 us -> 30.1 us (level)
  no operation moved by 1% of the time
where the time goes in v5:
time: 30.1 us; the launch traced here: 29.8 us
  blocking collectives  24.6 us (82%)
  Pallas kernels  2.96 us (10%)
  waiting for transfers between devices  1.11 us (4%)
  between operations  0.67 us (2%)
  starting transfers between devices  0.33 us (1%)
    all_to_all x1, blocking collectives, shards(): mine = lax.all_to_all(halves, AXES, 0, 0).reshape(-1, width + LANES)  15.5 us
    all_to_all x1, blocking collectives, shards(): stats = lax.all_to_all(local, AXES, 0, 0, tiled=True)  9.09 us
    pallas_call x1, Pallas kernels, shards(): pl.pallas_call(functools.partial(finish_kernel, rows * devices / groups,...  1.24 us
    ppermute x1, waiting for transfers between devices, shards(): other = lax.ppermute(mine, 'grp', [(i, i ^ 1) for i in range(grp)])  1.11 us
    pallas_call x1, Pallas kernels, shards(): pl.pallas_call(functools.partial(score_kernel, factor, groups), out_shape...  0.89 us
    pallas_call x1, Pallas kernels, shards(): pl.pallas_call(pack_kernel, out_shape=jax.ShapeDtypeStruct((2, own_caps /...  0.82 us
  transfers between devices with their start and end apart: 1, of which 1 were waited for; matrix products, arithmetic and copies ran while one was open for 0% of the time, Pallas kernels for 0%

profile of v5, /device:TPU:0, one launch (start us, length us, event | category | flops | bytes accessed | tf_op | source)
XLA Modules:
  0.0 29.8 jit_solution(17276016585817711855)
XLA Ops:
  0.6 0.0 copy-start
  0.6 0.8 %pack.1 = bf16[2,2,1152]{2,1,0:T(2,128)(2,1)S(1)} custom-call(s32[4]{0:T(128)} %ids_ref.1, bf16[4,1024]{1,0:T(4,128)(2,1)} %caps_ref.1), custom_call_target="tpu_custom_call" | custom-call | tf_op jit(solution)/shard_map/pack/pallas_call | solution.py:191
  1.5 0.1 broadcast_in_dim.2
  1.6 15.5 %all_to_all.16 = bf16[32,2,1152]{2,1,0:T(2,128)(2,1)S(1)} all-to-all(bf16[32,2,1152]{2,1,0:T(2,128)(2,1)S(1)} %bitcast.10), channel_id=1, replica_groups=mesh['dp'=8,'grp'=4] {'dp','grp'}, dimensions={0} | all-to-all | bytes 294912 | tf_op jit(solution)/shard_map/all_to_all | solution.py:206
  17.1 0.1 reshape.20.mine_ref
  17.2 0.0 copy-start.1
  17.2 0.3 %collective-permute-start = (bf16[64,1152]{1,0:T(8,128)(2,1)S(1)}, bf16[64,1152]{1,0:T(8,128)(2,1)S(1)}, u32[]{:S(2)}, u32[]{:S(2)}) collective-permute-start(bf16[64,1152]{1,0:T(8,128)(2,1)S(1)} %reshape.20.mine_ref), channel_id=1, source_target_pairs={{0,1},{1,0},{2,3},{3,2},{4,5},{5,4},{6,7},{7,6},{8,9},{9,8},{10,11... | collective-permute-start | bytes 442376 | tf_op jit(solution)/shard_map/ppermute | solution.py:207
  17.5 1.1 %collective-permute-done.other_ref = bf16[64,1152]{1,0:T(8,128)(2,1)S(1)} collective-permute-done((bf16[64,1152]{1,0:T(8,128)(2,1)S(1)}, bf16[64,1152]{1,0:T(8,128)(2,1)S(1)}, u32[]{:S(2)}, u32[]{:S(2)}) %collective-permute-start) | collective-permute-done | bytes 147488 | tf_op jit(solution)/shard_map/ppermute | solution.py:207
  18.6 0.0 copy-done
  18.6 0.0 copy-done.1
  18.6 0.9 %scores.1 = (f32[32,128]{1,0:T(8,128)S(1)}, f32[256,128]{1,0:T(8,128)S(1)}, f32[256,1024]{1,0:T(8,128)S(1)}, f32[256,1024]{1,0:T(8,128)S(1)}) custom-call(bf16[256,1024]{1,0:T(8,128)(2,1)S(1)} %copy-done, bf16[64,1152]{1,0:T(8,128)(2,1)S(1)} %reshape.20.mine_ref, bf16[64,1152]{1,0:T(8,128)(2,1)S(1)} %collective-permute-done.other_ref, s32[1,256]{1,0:T(1,128)S(1)} %bitcast.9), custom_call_target="tpu_custom_call" | custom-call | tf_op jit(solution)/shard_map/scores/pallas_call | solution.py:211
  19.5 9.1 %all_to_all.17 = f32[32,1,128]{2,1,0:T(1,128)S(1)} all-to-all(f32[32,1,128]{2,1,0:T(1,128)S(1)} %bitcast.7), channel_id=1, replica_groups=mesh['dp'=8,'grp'=4] {'dp','grp'}, dimensions={0} | all-to-all | bytes 32768 | tf_op jit(solution)/shard_map/all_to_all | solution.py:226
  28.6 1.2 %finish.1 = (f32[256,1024]{1,0:T(8,128)}, f32[1,8]{1,0:T(1,128)}) custom-call(f32[32,128]{1,0:T(8,128)S(1)} %bitcast.8, f32[32,128]{1,0:T(8,128)S(1)} %get-tuple-element.8.local_ref, f32[256,128]{1,0:T(8,128)S(1)} %get-tuple-element.9.lift_ref, f32[256,1024]{1,0:T(8,128)S(1)} %get-tuple-element.10.all_ref, f32[256,1024]{1,0:T(8,128)S(1)} %get-tuple-element.11.pos_ref), custom_call_target="tpu_custom_call" | custom-call | tf_op jit(solution)/shard_map/finish/pallas_call | solution.py:229
Async XLA Ops:
  0.6 18.0 %copy-start = (bf16[256,1024]{1,0:T(8,128)(2,1)S(1)}, bf16[256,1024]{1,0:T(8,128)(2,1)}, u32[]{:S(2)}) copy-start(bf16[256,1024]{1,0:T(8,128)(2,1)} %clips_ref.1) | copy-start | bytes 1572868
  17.2 1.5 %copy-start.1 = (s32[256]{0:T(256)S(1)}, s32[256]{0:T(256)}, u32[]{:S(2)}) copy-start(s32[256]{0:T(256)} %param.6) | copy-start | bytes 3076
  17.2 1.4 %collective-permute-start = (bf16[64,1152]{1,0:T(8,128)(2,1)S(1)}, bf16[64,1152]{1,0:T(8,128)(2,1)S(1)}, u32[]{:S(2)}, u32[]{:S(2)}) collective-permute-start(bf16[64,1152]{1,0:T(8,128)(2,1)S(1)} %reshape.20.mine_ref), channel_id=1, source_target_pairs={{0,1},{1,0},{2,3},{3,2},{4,5},{5,4},{6,7},{7,6},{8,9},{9,8},{10,11... | collective-permute-start | bytes 442376 | tf_op jit(solution)/shard_map/ppermute | solution.py:207

commit v6 on v5

--- a/solution.py
+++ b/solution.py
@@ -15,7 +15,12 @@
 LANES = 128
 ROW_CHUNK = 128
 VMEM = pl.BlockSpec(memory_space=pltpu.VMEM)
+ANY = pl.BlockSpec(memory_space=pl.ANY)
 HBM = pl.BlockSpec(memory_space=pltpu.HBM)
+
+
+def in_hbm(array):
+    return pltpu.with_memory_space_constraint(array, pltpu.HBM)
 
 
 def score_kernel(
@@ -99,6 +104,17 @@
     stats_ref[...] = jnp.broadcast_to(jnp.where(is_top, local_top, sums), stats_ref.shape)
 
 
+def fetch_kernel(clips_ref, group_ref, after_ref, clips_out, group_out, sems):
+    copies = [
+        pltpu.make_async_copy(clips_ref, clips_out, sems.at[0]),
+        pltpu.make_async_copy(group_ref, group_out, sems.at[1]),
+    ]
+    for copy in copies:
+        copy.start()
+    for copy in copies:
+        copy.wait()
+
+
 def pack_kernel(ids_ref, caps_ref, packed_ref, caps, ids, sems):
     copies = [
         pltpu.make_async_copy(ids_ref, ids, sems.at[0]),
@@ -200,12 +216,27 @@
         ],
         compiler_params=pltpu.CompilerParams(vmem_limit_bytes=1 << 20),
         name="pack",
-    )(*[pltpu.with_memory_space_constraint(a, pltpu.HBM) for a in (caption_group, captions)])
+    )(in_hbm(caption_group), in_hbm(captions))
     halves = jnp.broadcast_to(halves[None], (devices // 2,) + halves.shape)
     halves = halves.reshape(devices, own_caps // 2, width + LANES)
     mine = lax.all_to_all(halves, AXES, 0, 0).reshape(-1, width + LANES)
     other = lax.ppermute(mine, "grp", [(i, i ^ 1) for i in range(grp)])
 
+    clips, group_row = pl.pallas_call(
+        fetch_kernel,
+        out_shape=[
+            jax.ShapeDtypeStruct(clips.shape, clips.dtype),
+            jax.ShapeDtypeStruct((1, rows), clip_group.dtype),
+        ],
+        in_specs=[HBM, HBM, ANY],
+        out_specs=[VMEM] * 2,
+        scratch_shapes=[pltpu.SemaphoreType.DMA((2,))],
+        compiler_params=pltpu.CompilerParams(vmem_limit_bytes=1 << 20),
+        cost_estimate=pl.CostEstimate(
+            flops=0, bytes_accessed=4 * clips.size, transcendentals=0
+        ),
+        name="fetch",
+    )(in_hbm(clips), in_hbm(clip_group.reshape(1, rows)), mine)
     grant = (6 << 20) + 24 * rows * own_caps * devices
     f32 = functools.partial(jax.ShapeDtypeStruct, dtype=jnp.float32)
     local, lifts, all_part, pos_part = pl.pallas_call(
@@ -221,7 +252,7 @@
         scratch_shapes=[pltpu.VMEM((own_caps * devices, width + LANES), jnp.bfloat16)],
         compiler_params=pltpu.CompilerParams(vmem_limit_bytes=grant),
         name="scores",
-    )(clips, mine, other, clip_group.reshape(1, rows))
+    )(clips, mine, other, group_row)
 
     stats = lax.all_to_all(local, AXES, 0, 0, tiled=True)
 

time: 30.1 us -> 30 us (level)
  waiting for transfers between devices: 1.11 us -> 0.04 us
  Pallas kernels: 2.96 us -> 3.92 us
    ppermute x1, waiting for transfers between devices: 1.11 us -> 0.04 us  [shards(): other = lax.ppermute(mine, 'grp', [(i, i ^ 1) for i in range(grp)])]
    pallas_call x0 -> x1, Pallas kernels: none -> 1.06 us  [shards(): pl.pallas_call(fetch_kernel, out_shape=[jax.ShapeDtypeStruct(clips.shape,...]
  transfers between devices with their start and end apart: 1 -> 1, of which waited for: 1 -> 0; matrix products, arithmetic and copies ran while one was open for 0% -> 0% of each run, Pallas kernels for 0% -> 4%
where the time goes in v6:
time: 30 us; the launch traced here: 29.7 us
  blocking collectives  24.6 us (82%)
  Pallas kernels  3.92 us (13%)
  between operations  0.66 us (2%)
  starting transfers between devices  0.33 us (1%)
    all_to_all x1, blocking collectives, shards(): mine = lax.all_to_all(halves, AXES, 0, 0).reshape(-1, width + LANES)  15.5 us
    all_to_all x1, blocking collectives, shards(): stats = lax.all_to_all(local, AXES, 0, 0, tiled=True)  9.09 us
    pallas_call x1, Pallas kernels, shards(): pl.pallas_call(functools.partial(finish_kernel, rows * devices / groups,...  1.24 us
    pallas_call x1, Pallas kernels, shards(): pl.pallas_call(fetch_kernel, out_shape=[jax.ShapeDtypeStruct(clips.shape,...  1.06 us
    pallas_call x1, Pallas kernels, shards(): pl.pallas_call(functools.partial(score_kernel, factor, groups), out_shape...  0.89 us
    pallas_call x1, Pallas kernels, shards(): pl.pallas_call(pack_kernel, out_shape=jax.ShapeDtypeStruct((2, own_caps /...  0.73 us
  transfers between devices with their start and end apart: 1, of which 0 were waited for; matrix products, arithmetic and copies ran while one was open for 0% of the time, Pallas kernels for 4%

profile of v6, /device:TPU:0, one launch (start us, length us, event | category | flops | bytes accessed | tf_op | source)
XLA Modules:
  0.0 29.7 jit_solution(2969230407036872525)
XLA Ops:
  0.6 0.7 %pack.1 = bf16[2,2,1152]{2,1,0:T(2,128)(2,1)S(1)} custom-call(s32[4]{0:T(128)} %ids_ref.1, bf16[4,1024]{1,0:T(4,128)(2,1)} %caps_ref.1), custom_call_target="tpu_custom_call" | custom-call | tf_op jit(solution)/shard_map/pack/pallas_call | solution.py:207
  1.4 0.1 broadcast_in_dim.2
  1.5 15.5 %all_to_all.16 = bf16[32,2,1152]{2,1,0:T(2,128)(2,1)S(1)} all-to-all(bf16[32,2,1152]{2,1,0:T(2,128)(2,1)S(1)} %bitcast.9), channel_id=1, replica_groups=mesh['dp'=8,'grp'=4] {'dp','grp'}, dimensions={0} | all-to-all | bytes 294912 | tf_op jit(solution)/shard_map/all_to_all | solution.py:222
  17.0 0.1 reshape.21.after_ref.mine_ref
  17.1 0.3 %collective-permute-start = (bf16[64,1152]{1,0:T(8,128)(2,1)S(1)}, bf16[64,1152]{1,0:T(8,128)(2,1)S(1)}, u32[]{:S(2)}, u32[]{:S(2)}) collective-permute-start(bf16[64,1152]{1,0:T(8,128)(2,1)S(1)} %reshape.21.after_ref.mine_ref), channel_id=1, source_target_pairs={{0,1},{1,0},{2,3},{3,2},{4,5},{5,4},{6,7},{7,6},{8,9},{9,8},{10,11... | collective-permute-start | bytes 442376 | tf_op jit(solution)/shard_map/ppermute | solution.py:223
  17.4 1.1 %fetch.1 = (bf16[256,1024]{1,0:T(8,128)(2,1)S(1)}, s32[1,256]{1,0:T(1,128)S(1)}) custom-call(bf16[256,1024]{1,0:T(8,128)(2,1)} %clips_ref.1, s32[1,256]{1,0:T(1,128)} %bitcast.10, bf16[64,1152]{1,0:T(8,128)(2,1)S(1)} %reshape.21.after_ref.mine_ref), custom_call_target="tpu_custom_call" | custom-call | bytes 1048576 | tf_op jit(solution)/shard_map/fetch/pallas_call | solution.py:225
  18.5 0.0 collective-permute-done.other_ref
  18.5 0.9 %scores.1 = (f32[32,128]{1,0:T(8,128)S(1)}, f32[256,128]{1,0:T(8,128)S(1)}, f32[256,1024]{1,0:T(8,128)S(1)}, f32[256,1024]{1,0:T(8,128)S(1)}) custom-call(bf16[256,1024]{1,0:T(8,128)(2,1)S(1)} %get-tuple-element.10.clips_ref, bf16[64,1152]{1,0:T(8,128)(2,1)S(1)} %reshape.21.after_ref.mine_ref, bf16[64,1152]{1,0:T(8,128)(2,1)S(1)} %collective-permute-done.other_ref, ...), custom_call_target="tpu_custom_call" | custom-call | tf_op jit(solution)/shard_map/scores/pallas_call | solution.py:242
  19.4 9.1 %all_to_all.17 = f32[32,1,128]{2,1,0:T(1,128)S(1)} all-to-all(f32[32,1,128]{2,1,0:T(1,128)S(1)} %bitcast.7), channel_id=1, replica_groups=mesh['dp'=8,'grp'=4] {'dp','grp'}, dimensions={0} | all-to-all | bytes 32768 | tf_op jit(solution)/shard_map/all_to_all | solution.py:257
  28.5 1.2 %finish.1 = (f32[256,1024]{1,0:T(8,128)}, f32[1,8]{1,0:T(1,128)}) custom-call(f32[32,128]{1,0:T(8,128)S(1)} %bitcast.8, f32[32,128]{1,0:T(8,128)S(1)} %get-tuple-element.12.local_ref, f32[256,128]{1,0:T(8,128)S(1)} %get-tuple-element.13.lift_ref, f32[256,1024]{1,0:T(8,128)S(1)} %get-tuple-element.14.all_ref, f32[256,1024]{1,0:T(8,128)S(1)} %get-tuple-element.15.pos_ref), custom_call_target="tpu_custom_call" | custom-call | tf_op jit(solution)/shard_map/finish/pallas_call | solution.py:260
Async XLA Ops:
  17.1 1.4 %collective-permute-start = (bf16[64,1152]{1,0:T(8,128)(2,1)S(1)}, bf16[64,1152]{1,0:T(8,128)(2,1)S(1)}, u32[]{:S(2)}, u32[]{:S(2)}) collective-permute-start(bf16[64,1152]{1,0:T(8,128)(2,1)S(1)} %reshape.21.after_ref.mine_ref), channel_id=1, source_target_pairs={{0,1},{1,0},{2,3},{3,2},{4,5},{5,4},{6,7},{7,6},{8,9},{9,8},{10,11... | collective-permute-start | bytes 442376 | tf_op jit(solution)/shard_map/ppermute | solution.py:223

commit v7 on v6

--- a/solution.py
+++ b/solution.py
@@ -14,6 +14,7 @@
 ID_BASE = 1 << ID_BITS
 LANES = 128
 ROW_CHUNK = 128
+GRAD_COPIES = 4
 VMEM = pl.BlockSpec(memory_space=pltpu.VMEM)
 ANY = pl.BlockSpec(memory_space=pl.ANY)
 HBM = pl.BlockSpec(memory_space=pltpu.HBM)
@@ -143,7 +144,6 @@
 def finish_kernel(
     scale,
     groups,
-    chunk,
     stats_ref,
     local_ref,
     lift_ref,
@@ -173,8 +173,9 @@
 
     rows = all_ref.shape[0]
     copies = []
-    for index, start in enumerate(range(0, rows, chunk)):
-        part = slice(start, start + chunk)
+    bounds = [0, rows // 16, rows // 4, rows // 2, rows]
+    for index, (start, stop) in enumerate(zip(bounds, bounds[1:])):
+        part = slice(start, stop)
         own = lift_ref[part, :]
         gain_all = jnp.sum(own * gains_all, axis=1, keepdims=True)
         gain_pos = jnp.sum(own * gains_pos, axis=1, keepdims=True)
@@ -256,16 +257,15 @@
 
     stats = lax.all_to_all(local, AXES, 0, 0, tiled=True)
 
-    chunk = rows // 8
     clip_grad, group_loss = pl.pallas_call(
-        functools.partial(finish_kernel, rows * devices / groups, groups, chunk),
+        functools.partial(finish_kernel, rows * devices / groups, groups),
         out_shape=[f32((rows, width)), f32((1, groups // grp))],
         in_specs=[VMEM] * 5,
         out_specs=[HBM, HBM],
         scratch_shapes=[
             pltpu.VMEM((rows, width), jnp.float32),
             pltpu.VMEM((1, groups // grp), jnp.float32),
-            pltpu.SemaphoreType.DMA((rows // chunk,)),
+            pltpu.SemaphoreType.DMA((GRAD_COPIES,)),
             pltpu.SemaphoreType.DMA,
         ],
         compiler_params=pltpu.CompilerParams(vmem_limit_bytes=grant),

time: 30 us -> 29.9 us (level)
  no operation moved by 1% of the time
where the time goes in v7:
time: 29.9 us; the launch traced here: 29.7 us
  blocking collectives  24.6 us (82%)
  Pallas kernels  3.89 us (13%)
  between operations  0.66 us (2%)
  starting transfers between devices  0.33 us (1%)
    all_to_all x1, blocking collectives, shards(): mine = lax.all_to_all(halves, AXES, 0, 0).reshape(-1, width + LANES)  15.5 us
    all_to_all x1, blocking collectives, shards(): stats = lax.all_to_all(local, AXES, 0, 0, tiled=True)  9.09 us
    pallas_call x1, Pallas kernels, shards(): pl.pallas_call(functools.partial(finish_kernel, rows * devices / groups,...  1.22 us
    pallas_call x1, Pallas kernels, shards(): pl.pallas_call(fetch_kernel, out_shape=[jax.ShapeDtypeStruct(clips.shape,...  1.06 us
    pallas_call x1, Pallas kernels, shards(): pl.pallas_call(functools.partial(score_kernel, factor, groups), out_shape...  0.89 us
    pallas_call x1, Pallas kernels, shards(): pl.pallas_call(pack_kernel, out_shape=jax.ShapeDtypeStruct((2, own_caps /...  0.73 us
  transfers between devices with their start and end apart: 1, of which 0 were waited for; matrix products, arithmetic and copies ran while one was open for 0% of the time, Pallas kernels for 4%

profile of v7, /device:TPU:0, one launch (start us, length us, event | category | flops | bytes accessed | tf_op | source)
XLA Modules:
  0.0 29.7 jit_solution(6243419473500341746)
XLA Ops:
  0.6 0.7 %pack.1 = bf16[2,2,1152]{2,1,0:T(2,128)(2,1)S(1)} custom-call(s32[4]{0:T(128)} %ids_ref.1, bf16[4,1024]{1,0:T(4,128)(2,1)} %caps_ref.1), custom_call_target="tpu_custom_call" | custom-call | tf_op jit(solution)/shard_map/pack/pallas_call | solution.py:208
  1.4 0.1 broadcast_in_dim.2
  1.5 15.5 %all_to_all.16 = bf16[32,2,1152]{2,1,0:T(2,128)(2,1)S(1)} all-to-all(bf16[32,2,1152]{2,1,0:T(2,128)(2,1)S(1)} %bitcast.9), channel_id=1, replica_groups=mesh['dp'=8,'grp'=4] {'dp','grp'}, dimensions={0} | all-to-all | bytes 294912 | tf_op jit(solution)/shard_map/all_to_all | solution.py:223
  17.0 0.1 reshape.21.after_ref.mine_ref
  17.1 0.3 %collective-permute-start = (bf16[64,1152]{1,0:T(8,128)(2,1)S(1)}, bf16[64,1152]{1,0:T(8,128)(2,1)S(1)}, u32[]{:S(2)}, u32[]{:S(2)}) collective-permute-start(bf16[64,1152]{1,0:T(8,128)(2,1)S(1)} %reshape.21.after_ref.mine_ref), channel_id=1, source_target_pairs={{0,1},{1,0},{2,3},{3,2},{4,5},{5,4},{6,7},{7,6},{8,9},{9,8},{10,11... | collective-permute-start | bytes 442376 | tf_op jit(solution)/shard_map/ppermute | solution.py:224
  17.4 1.1 %fetch.1 = (bf16[256,1024]{1,0:T(8,128)(2,1)S(1)}, s32[1,256]{1,0:T(1,128)S(1)}) custom-call(bf16[256,1024]{1,0:T(8,128)(2,1)} %clips_ref.1, s32[1,256]{1,0:T(1,128)} %bitcast.10, bf16[64,1152]{1,0:T(8,128)(2,1)S(1)} %reshape.21.after_ref.mine_ref), custom_call_target="tpu_custom_call" | custom-call | bytes 1048576 | tf_op jit(solution)/shard_map/fetch/pallas_call | solution.py:226
  18.5 0.0 collective-permute-done.other_ref
  18.5 0.9 %scores.1 = (f32[32,128]{1,0:T(8,128)S(1)}, f32[256,128]{1,0:T(8,128)S(1)}, f32[256,1024]{1,0:T(8,128)S(1)}, f32[256,1024]{1,0:T(8,128)S(1)}) custom-call(bf16[256,1024]{1,0:T(8,128)(2,1)S(1)} %get-tuple-element.10.clips_ref, bf16[64,1152]{1,0:T(8,128)(2,1)S(1)} %reshape.21.after_ref.mine_ref, bf16[64,1152]{1,0:T(8,128)(2,1)S(1)} %collective-permute-done.other_ref, ...), custom_call_target="tpu_custom_call" | custom-call | tf_op jit(solution)/shard_map/scores/pallas_call | solution.py:243
  19.4 9.1 %all_to_all.17 = f32[32,1,128]{2,1,0:T(1,128)S(1)} all-to-all(f32[32,1,128]{2,1,0:T(1,128)S(1)} %bitcast.7), channel_id=1, replica_groups=mesh['dp'=8,'grp'=4] {'dp','grp'}, dimensions={0} | all-to-all | bytes 32768 | tf_op jit(solution)/shard_map/all_to_all | solution.py:258
  28.5 1.2 %finish.1 = (f32[256,1024]{1,0:T(8,128)}, f32[1,8]{1,0:T(1,128)}) custom-call(f32[32,128]{1,0:T(8,128)S(1)} %bitcast.8, f32[32,128]{1,0:T(8,128)S(1)} %get-tuple-element.12.local_ref, f32[256,128]{1,0:T(8,128)S(1)} %get-tuple-element.13.lift_ref, f32[256,1024]{1,0:T(8,128)S(1)} %get-tuple-element.14.all_ref, f32[256,1024]{1,0:T(8,128)S(1)} %get-tuple-element.15.pos_ref), custom_call_target="tpu_custom_call" | custom-call | tf_op jit(solution)/shard_map/finish/pallas_call | solution.py:260
Async XLA Ops:
  17.1 1.4 %collective-permute-start = (bf16[64,1152]{1,0:T(8,128)(2,1)S(1)}, bf16[64,1152]{1,0:T(8,128)(2,1)S(1)}, u32[]{:S(2)}, u32[]{:S(2)}) collective-permute-start(bf16[64,1152]{1,0:T(8,128)(2,1)S(1)} %reshape.21.after_ref.mine_ref), channel_id=1, source_target_pairs={{0,1},{1,0},{2,3},{3,2},{4,5},{5,4},{6,7},{7,6},{8,9},{9,8},{10,11... | collective-permute-start | bytes 442376 | tf_op jit(solution)/shard_map/ppermute | solution.py:224

commit v8 on v7

--- a/solution.py
+++ b/solution.py
@@ -25,12 +25,10 @@
 
 
 def score_kernel(
-    factor, groups, clips_ref, mine_ref, other_ref, group_ref, stats_ref, lift_ref, all_ref, pos_ref, caps
+    factor, groups, clips_ref, mine_ref, other_ref, group_ref, stats_ref, lift_ref, all_ref, pos_ref
 ):
     rows, width = clips_ref.shape
-    half = mine_ref.shape[0]
-    caps[:half, :] = mine_ref[...]
-    caps[half:, :] = other_ref[...]
+    caps = jnp.concatenate([mine_ref[...], other_ref[...]], axis=0)
 
     weigh_digit = lax.broadcasted_iota(jnp.int32, (8, LANES), 1)
     weigh_digit = jnp.where(weigh_digit == 0, float(ID_BASE), jnp.where(weigh_digit == 1, 1.0, 0.0))
@@ -250,7 +248,6 @@
         ],
         in_specs=[VMEM] * 4,
         out_specs=[VMEM] * 4,
-        scratch_shapes=[pltpu.VMEM((own_caps * devices, width + LANES), jnp.bfloat16)],
         compiler_params=pltpu.CompilerParams(vmem_limit_bytes=grant),
         name="scores",
     )(clips, mine, other, group_row)

time: 29.9 us -> 30 us (level)
  no operation moved by 1% of the time
where the time goes in v8:
time: 30 us; the launch traced here: 29.7 us
  blocking collectives  24.6 us (82%)
  Pallas kernels  3.93 us (13%)
  between operations  0.67 us (2%)
  starting transfers between devices  0.33 us (1%)
    all_to_all x1, blocking collectives, shards(): mine = lax.all_to_all(halves, AXES, 0, 0).reshape(-1, width + LANES)  15.5 us
    all_to_all x1, blocking collectives, shards(): stats = lax.all_to_all(local, AXES, 0, 0, tiled=True)  9.08 us
    pallas_call x1, Pallas kernels, shards(): pl.pallas_call(functools.partial(finish_kernel, rows * devices / groups,...  1.22 us
    pallas_call x1, Pallas kernels, shards(): pl.pallas_call(fetch_kernel, out_shape=[jax.ShapeDtypeStruct(clips.shape,...  1.06 us
    pallas_call x1, Pallas kernels, shards(): pl.pallas_call(functools.partial(score_kernel, factor, groups), out_shape...  0.92 us
    pallas_call x1, Pallas kernels, shards(): pl.pallas_call(pack_kernel, out_shape=jax.ShapeDtypeStruct((2, own_caps /...  0.73 us
  transfers between devices with their start and end apart: 1, of which 0 were waited for; matrix products, arithmetic and copies ran while one was open for 0% of the time, Pallas kernels for 4%

profile of v8, /device:TPU:0, one launch (start us, length us, event | category | flops | bytes accessed | tf_op | source)
XLA Modules:
  0.0 29.7 jit_solution(2870389044622244123)
XLA Ops:
  0.6 0.7 %pack.1 = bf16[2,2,1152]{2,1,0:T(2,128)(2,1)S(1)} custom-call(s32[4]{0:T(128)} %ids_ref.1, bf16[4,1024]{1,0:T(4,128)(2,1)} %caps_ref.1), custom_call_target="tpu_custom_call" | custom-call | tf_op jit(solution)/shard_map/pack/pallas_call | solution.py:206
  1.4 0.1 broadcast_in_dim.2
  1.5 15.5 %all_to_all.16 = bf16[32,2,1152]{2,1,0:T(2,128)(2,1)S(1)} all-to-all(bf16[32,2,1152]{2,1,0:T(2,128)(2,1)S(1)} %bitcast.9), channel_id=1, replica_groups=mesh['dp'=8,'grp'=4] {'dp','grp'}, dimensions={0} | all-to-all | bytes 294912 | tf_op jit(solution)/shard_map/all_to_all | solution.py:221
  17.0 0.1 reshape.21.after_ref.mine_ref
  17.1 0.3 %collective-permute-start = (bf16[64,1152]{1,0:T(8,128)(2,1)S(1)}, bf16[64,1152]{1,0:T(8,128)(2,1)S(1)}, u32[]{:S(2)}, u32[]{:S(2)}) collective-permute-start(bf16[64,1152]{1,0:T(8,128)(2,1)S(1)} %reshape.21.after_ref.mine_ref), channel_id=1, source_target_pairs={{0,1},{1,0},{2,3},{3,2},{4,5},{5,4},{6,7},{7,6},{8,9},{9,8},{10,11... | collective-permute-start | bytes 442376 | tf_op jit(solution)/shard_map/ppermute | solution.py:222
  17.4 1.1 %fetch.1 = (bf16[256,1024]{1,0:T(8,128)(2,1)S(1)}, s32[1,256]{1,0:T(1,128)S(1)}) custom-call(bf16[256,1024]{1,0:T(8,128)(2,1)} %clips_ref.1, s32[1,256]{1,0:T(1,128)} %bitcast.10, bf16[64,1152]{1,0:T(8,128)(2,1)S(1)} %reshape.21.after_ref.mine_ref), custom_call_target="tpu_custom_call" | custom-call | bytes 1048576 | tf_op jit(solution)/shard_map/fetch/pallas_call | solution.py:224
  18.5 0.0 collective-permute-done.other_ref
  18.5 0.9 %scores.1 = (f32[32,128]{1,0:T(8,128)S(1)}, f32[256,128]{1,0:T(8,128)S(1)}, f32[256,1024]{1,0:T(8,128)S(1)}, f32[256,1024]{1,0:T(8,128)S(1)}) custom-call(bf16[256,1024]{1,0:T(8,128)(2,1)S(1)} %get-tuple-element.10.clips_ref, bf16[64,1152]{1,0:T(8,128)(2,1)S(1)} %reshape.21.after_ref.mine_ref, bf16[64,1152]{1,0:T(8,128)(2,1)S(1)} %collective-permute-done.other_ref, ...), custom_call_target="tpu_custom_call" | custom-call | tf_op jit(solution)/shard_map/scores/pallas_call | solution.py:241
  19.4 9.1 %all_to_all.17 = f32[32,1,128]{2,1,0:T(1,128)S(1)} all-to-all(f32[32,1,128]{2,1,0:T(1,128)S(1)} %bitcast.7), channel_id=1, replica_groups=mesh['dp'=8,'grp'=4] {'dp','grp'}, dimensions={0} | all-to-all | bytes 32768 | tf_op jit(solution)/shard_map/all_to_all | solution.py:255
  28.5 1.2 %finish.1 = (f32[256,1024]{1,0:T(8,128)}, f32[1,8]{1,0:T(1,128)}) custom-call(f32[32,128]{1,0:T(8,128)S(1)} %bitcast.8, f32[32,128]{1,0:T(8,128)S(1)} %get-tuple-element.12.local_ref, f32[256,128]{1,0:T(8,128)S(1)} %get-tuple-element.13.lift_ref, f32[256,1024]{1,0:T(8,128)S(1)} %get-tuple-element.14.all_ref, f32[256,1024]{1,0:T(8,128)S(1)} %get-tuple-element.15.pos_ref), custom_call_target="tpu_custom_call" | custom-call | tf_op jit(solution)/shard_map/finish/pallas_call | solution.py:257
Async XLA Ops:
  17.1 1.4 %collective-permute-start = (bf16[64,1152]{1,0:T(8,128)(2,1)S(1)}, bf16[64,1152]{1,0:T(8,128)(2,1)S(1)}, u32[]{:S(2)}, u32[]{:S(2)}) collective-permute-start(bf16[64,1152]{1,0:T(8,128)(2,1)S(1)} %reshape.21.after_ref.mine_ref), channel_id=1, source_target_pairs={{0,1},{1,0},{2,3},{3,2},{4,5},{5,4},{6,7},{7,6},{8,9},{9,8},{10,11... | collective-permute-start | bytes 442376 | tf_op jit(solution)/shard_map/ppermute | solution.py:222
